TPU v7x, 128 devices: a whole 4x4x4 slice. The times are simulated.
128 devices in a mesh: phrase: 16 (over y, z_lo, core), vocab: 8 (over x, z_hi).
Axes of the slice: x: 4, y: 4, z: 4 (z_hi: 2, z_lo: 2; z = z_hi * 2 + z_lo), core: 2. Of those that a mesh axis runs over, the one named last changes fastest.
Arguments:
- frames: bfloat16 [1536, 1024], P(('phrase', 'vocab'))
- frame_lens: int32 [4], replicated, may hold values from 192 to 384, as said below
- labels: int32 [4, 64], replicated, may hold values from 1 to 4095
- label_lens: int32 [4], replicated, may hold values from 16 to 63, as said below
- phrase_ids: int32 [65536, 8], P(('phrase', 'vocab')), may hold values from 0 to 4095
- phrase_lens: int32 [65536], P(('phrase', 'vocab')), may hold values from 1 to 8
- phrase_table: bfloat16 [4096, 512], replicated, may hold values from -6 to 6
- phrase_w: bfloat16 [512, 512], replicated, may hold values from -0.25 to 0.25
- key_w: bfloat16 [512, 512], replicated, may hold values from -0.25 to 0.25
- value_w: bfloat16 [512, 512], replicated, may hold values from -0.25 to 0.25
- query_w: bfloat16 [1024, 512], replicated, may hold values from -0.9375 to 0.9375
- context_w: bfloat16 [512, 1024], replicated, may hold values from -0.25 to 0.25
- joint_enc_w: bfloat16 [1024, 640], replicated, may hold values from -0.1875 to 0.1875
- pred_table: bfloat16 [4096, 640], replicated, may hold values from -6 to 6
- pred_w: bfloat16 [640, 640], replicated, may hold values from -0.25 to 0.25
- out_w: bfloat16 [640, 4096], P(None, 'vocab')
Outputs:
- blank_logp: float32 [1536, 64], P('phrase', 'vocab')
- label_logp: float32 [1536, 64], P('phrase', 'vocab')
Inputs may be any that keep to these rules, and one draw needn't show every extreme that they name: `frame_lens`: some utterance has exactly 384 frames. `label_lens`: some utterance has exactly 63 labels.
All inputs are finite; a program needn't handle non-finite values.
Results may differ from a plain program's by a relative error of at most 0.0034.
Values may be sent and summed in bfloat16 or wider, within the bound.
No kernel may reach another device: no remote copies, remote signals or barrier semaphores. Data moves between devices by JAX's collectives and lax.ppermute only.
A program may use at most 128 MiB of HBM per device.

v0:
```python
import math

import jax
import jax.numpy as jnp
from jax import lax
from jax.sharding import PartitionSpec as P

HEADS = 4


def encode_local(ids, lens, phrase_table, phrase_w):
    emb = phrase_table[ids]
    mask = (jnp.arange(ids.shape[1], dtype=jnp.int32)[None, :] < lens[:, None]).astype(jnp.bfloat16)
    summed = jnp.einsum("npe,np->ne", emb, mask, preferred_element_type=jnp.float32)
    mean = (summed / lens[:, None].astype(jnp.float32)).astype(jnp.bfloat16)
    return jnp.tanh(jnp.dot(mean, phrase_w, preferred_element_type=jnp.float32)).astype(
        jnp.bfloat16
    )


def block_sums(asked, keys, values, blocks):
    head_size = keys.shape[1] // HEADS
    query_heads = asked.reshape(asked.shape[0], HEADS, head_size)
    key_heads = keys.reshape(keys.shape[0], HEADS, head_size)
    scores = jnp.einsum("fhd,phd->fhp", query_heads, key_heads, preferred_element_type=jnp.float32)
    scores = (scores * (1.0 / math.sqrt(head_size))).reshape(
        asked.shape[0], HEADS, blocks, keys.shape[0] // blocks
    )
    block_peak = jnp.max(scores, -1)
    weights = jnp.exp(scores - block_peak[..., None]).astype(jnp.bfloat16)
    block_total = jnp.sum(weights, -1, dtype=jnp.float32)
    value_heads = values.reshape(blocks, values.shape[0] // blocks, HEADS, head_size)
    block_numer = jnp.einsum(
        "fhbp,bphd->fhbd", weights, value_heads, preferred_element_type=jnp.float32
    )
    return (block_peak, block_total, block_numer)


def rescale(block_peak, block_total, block_numer, peak):
    factor = jnp.exp(block_peak - peak[..., None])
    return (jnp.sum(block_total * factor, -1), jnp.sum(block_numer * factor[..., None], 2))


def local(
    frames,
    frame_lens,
    labels,
    label_lens,
    phrase_ids,
    phrase_lens,
    phrase_table,
    phrase_w,
    key_w,
    value_w,
    query_w,
    context_w,
    joint_enc_w,
    pred_table,
    pred_w,
    out_w,
):
    phrase_vec = encode_local(phrase_ids, phrase_lens, phrase_table, phrase_w)
    keys = jnp.dot(phrase_vec, key_w, preferred_element_type=jnp.float32).astype(jnp.bfloat16)
    values = jnp.dot(phrase_vec, value_w, preferred_element_type=jnp.float32).astype(jnp.bfloat16)
    queries = jnp.dot(frames, query_w, preferred_element_type=jnp.float32).astype(jnp.bfloat16)
    asked = lax.all_gather(queries, ("phrase", "vocab"), axis=0, tiled=True)
    block_peak, block_total, block_numer = block_sums(asked, keys, values, 1)
    peak = lax.pmax(jnp.max(block_peak, -1), ("phrase", "vocab"))
    total, numer = rescale(block_peak, block_total, block_numer, peak)
    total, numer = (
        lax.psum_scatter(total, ("phrase", "vocab"), scatter_dimension=0, tiled=True),
        lax.psum_scatter(numer, ("phrase", "vocab"), scatter_dimension=0, tiled=True),
    )
    context = (numer / total[..., None]).reshape(frames.shape[0], -1).astype(jnp.bfloat16)
    biased = (
        frames.astype(jnp.float32) + jnp.dot(context, context_w, preferred_element_type=jnp.float32)
    ).astype(jnp.bfloat16)
    joint_rows = jnp.dot(biased, joint_enc_w, preferred_element_type=jnp.float32).astype(
        jnp.bfloat16
    )
    joint_all = lax.all_gather(joint_rows, "vocab", axis=0, tiled=True)
    n_vocab = lax.axis_size("vocab")
    vocab_index = lax.axis_index("vocab")
    utts, positions = labels.shape
    own = positions // n_vocab
    width = pred_w.shape[0]
    own_labels = lax.dynamic_slice_in_dim(labels, vocab_index * own, own, 1)
    step_rows = (
        jnp.dot(pred_table[own_labels.reshape(-1)], pred_w, preferred_element_type=jnp.float32)
        .astype(jnp.bfloat16)
        .reshape(utts, own, width)
    )
    step_all = lax.all_gather(step_rows, "vocab", axis=1, tiled=True)
    blank_row = jnp.dot(pred_table[0:1], pred_w, preferred_element_type=jnp.float32).astype(
        jnp.bfloat16
    )
    predictor = jnp.concatenate(
        [jnp.broadcast_to(blank_row[None], (utts, 1, width)), step_all[:, :-1]], 1
    )
    frames_dev = joint_all.shape[0]
    tlen = frames_dev * lax.axis_size("phrase") // utts
    global_index = lax.axis_index("phrase") * frames_dev + jnp.arange(frames_dev, dtype=jnp.int32)
    owner = global_index // tlen
    moment = global_index % tlen
    member = owner[:, None] == jnp.arange(utts, dtype=jnp.int32)[None, :]
    pred_sel = jnp.einsum(
        "fb,buh->fuh", member.astype(jnp.bfloat16), predictor, preferred_element_type=jnp.float32
    )
    joint_in = (
        jnp.tanh(joint_all[:, None, :].astype(jnp.float32) + pred_sel)
        .astype(jnp.bfloat16)
        .reshape(-1, width)
    )
    logits = jnp.dot(joint_in, out_w, preferred_element_type=jnp.float32)
    cols = out_w.shape[1]
    row_labels = jnp.sum(jnp.where(member[:, :, None], labels[None, :, :], 0), 1)
    column = vocab_index * cols + jnp.arange(cols, dtype=jnp.int32)
    label_part = jnp.sum(
        jnp.where(column[None, :] == row_labels.reshape(-1, 1), logits, 0.0), -1
    ).reshape(frames_dev, positions)
    blank_part = jnp.where(vocab_index == 0, logits[:, 0], 0.0).reshape(frames_dev, positions)
    start_own = vocab_index * own
    peak_rows = lax.pmax(jnp.max(logits, -1), "vocab")
    total_part = jnp.sum(jnp.exp(logits - peak_rows[:, None]), -1).reshape(frames_dev, positions)
    peak_own = lax.dynamic_slice_in_dim(peak_rows.reshape(frames_dev, positions), start_own, own, 1)
    total_every = lax.psum(total_part, "vocab")
    total_own = lax.dynamic_slice_in_dim(total_every, start_own, own, 1)
    blank_own, label_own = (
        lax.psum_scatter(blank_part, "vocab", scatter_dimension=1, tiled=True),
        lax.psum_scatter(label_part, "vocab", scatter_dimension=1, tiled=True),
    )
    norm = peak_own + jnp.log(total_own)
    positions_own = start_own + jnp.arange(own, dtype=jnp.int32)
    frame_len = jnp.sum(jnp.where(member, frame_lens[None, :], 0), 1)
    label_len = jnp.sum(jnp.where(member, label_lens[None, :], 0), 1)
    live = (moment < frame_len)[:, None]
    blank_out = jnp.where(
        live & (positions_own[None, :] <= label_len[:, None]), blank_own - norm, 0.0
    )
    label_out = jnp.where(
        live & (positions_own[None, :] < label_len[:, None]), label_own - norm, 0.0
    )
    return (blank_out, label_out)


def solution(mesh):
    in_specs = (
        P(("phrase", "vocab"), None),
        P(),
        P(),
        P(),
        P(("phrase", "vocab"), None),
        P(("phrase", "vocab")),
        P(),
        P(),
        P(),
        P(),
        P(),
        P(),
        P(),
        P(),
        P(),
        P(None, "vocab"),
    )
    out_specs = (P("phrase", "vocab"), P("phrase", "vocab"))
    return jax.shard_map(local, mesh=mesh, in_specs=in_specs, out_specs=out_specs, check_vma=False)
```

profile of v0, /device:TPU:0, one launch (start us, length us, event | category | flops | bytes accessed | tf_op | source)
XLA Modules:
  0.0 752.5 jit_solution(592532760997151571)
XLA Ops:
  7.2 2.2 fusion.14
  11.2 0.8 constant_dynamic-slice_fusion.1
  12.0 20.2 %gather_fusion = bf16[4096,512]{1,0:T(8,128)(2,1)} fusion(bf16[4096,512]{1,0:T(8,128)(2,1)} %param.22, s32[4096]{0:T(1024)S(1)} %broadcast_clamp_fusion), kind=kCustom, calls=%fused_computation | custom fusion | bytes 8404992 | tf_op jit(solution)/shard_map/gather | solution.py:12
  32.4 3.5 fusion.2
  36.9 1.3 convolution_convert_fusion.1
  38.2 274.2 %all-gather.4.cloned.1.call-done = bf16[128,12,512]{2,1,0:T(8,128)(2,1)} async-done(((bf16[1,12,512]{2,1,0:T(8,128)(2,1)}), bf16[128,12,512]{2,1,0:T(8,128)(2,1)}) %all-gather.4.cloned.1.call-update) | async-done | bytes 1572880 | tf_op jit(solution)/shard_map/all_gather | solution.py:66
  312.4 3.2 reshape.171
  315.6 6.4 bitcast_reduce_fusion
  322.1 66.9 %pmax.14 = f32[1536,4]{0,1:T(4,128)S(1)} all-reduce(f32[1536,4]{0,1:T(4,128)S(1)} %get-tuple-element.19), channel_id=1, replica_groups=mesh['phrase'=16,'vocab'=8] {'phrase','vocab'}, use_global_device_ids=true, to_apply=%region_3.0 | all-reduce | flops 6144 | bytes 49152 | tf_op jit(solution)/shard_map/pmax | solution.py:68
  389.0 6.8 convert_reduce_fusion
  396.4 0.7 copy-done.1
  397.2 5.0 fusion.5
  402.2 5.0 copy.48
  407.5 3.8 gather_fusion.1
  411.6 35.0 %all_gather.11 = bf16[4,64,640]{2,0,1:T(4,128)(2,1)S(1)} all-gather(bf16[4,8,640]{2,0,1:T(4,128)(2,1)S(1)} %copy.50), channel_id=1, replica_groups=mesh['phrase'=16,'vocab'=8] {'vocab'}, dimensions={1}, use_global_device_ids=true | all-gather | bytes 368640 | tf_op jit(solution)/shard_map/all_gather | solution.py:93
  448.0 0.8 copy.52
  449.5 1.2 dynamic-slice.2
  451.4 0.8 select_reduce_fusion.3
  452.2 0.9 convolution_reduce_fusion
  453.1 63.0 %all-reduce.1 = f32[1536,4]{0,1:T(4,128)S(1)} all-reduce(f32[1536,4]{0,1:T(4,128)} %get-tuple-element.15), channel_id=3, replica_groups=mesh['phrase'=16,'vocab'=8] {'phrase','vocab'}, use_global_device_ids=true, to_apply=%region_6.0.clone | all-reduce | flops 6144 | bytes 49152
  516.3 42.6 %all-reduce.8.cloned.1.call-done = f32[1536,4,128]{2,1,0:T(4,128)} async-done(((f32[1536,4,128]{2,1,0:T(4,128)}), f32[1536,4,128]{2,1,0:T(4,128)}) %all-reduce.8.cloned.1.call-update) | async-done | bytes 3145744
  558.9 0.8 fusion.28
  559.8 1.2 fusion.13
  561.0 34.2 %all-gather.1 = bf16[8,12,640]{2,1,0:T(8,128)(2,1)S(1)} all-gather(bf16[1,12,640]{2,1,0:T(8,128)(2,1)S(1)} %fusion.13), channel_id=1, replica_groups=mesh['phrase'=16,'vocab'=8] {'vocab'}, dimensions={0}, use_global_device_ids=true | all-gather | bytes 138240 | tf_op jit(solution)/shard_map/all_gather | solution.py:81
  595.3 3.6 tanh_convert_fusion
  598.9 6.0 copy.51
  605.0 11.2 %fusion.38 = (f32[6144]{0:T(1024)S(1)}, f32[6144,512]{0,1:T(8,128)}) fusion(bf16[6144,640]{1,0:T(8,128)(2,1)} %bitcast.74, bf16[640,512]{1,0:T(8,128)(2,1)S(1)} %copy-done.11), kind=kOutput, calls=%fused_computation.75 | convolution fusion | flops 4029671424 | bytes 21127168 | tf_op jit(solution)/shard_map/dot_general | solution.py:114
  616.2 40.3 %pmax.15 = f32[6144]{0:T(1024)S(1)} all-reduce(f32[6144]{0:T(1024)S(1)} %get-tuple-element.21), channel_id=1, replica_groups=mesh['phrase'=16,'vocab'=8] {'vocab'}, use_global_device_ids=true, to_apply=%region_9.10 | all-reduce | flops 6144 | bytes 49152 | tf_op jit(solution)/shard_map/pmax | solution.py:123
  656.6 6.5 select_reduce_fusion
  664.5 1.0 fusion.27
  666.3 77.4 %all-reduce.10.cloned.1.call-done = (f32[96,64]{1,0:T(8,128)}, f32[96,64]{1,0:T(8,128)}, f32[96,64]{1,0:T(8,128)}) async-done(((f32[96,64]{1,0:T(8,128)}, f32[96,64]{1,0:T(8,128)}, f32[96,64]{1,0:T(8,128)}), (f32[96,64]{1,0:T(8,128)}, f32[96,64]{1,0:T(8,128)}, f32[96,64]{1,0:T(8,128)})) %all-reduce.10.cloned.1.call-update) | async-done | bytes 73744
  743.7 1.0 fusion.25
  (65 shorter events, 9.9 us)
Async XLA Ops:
  7.2 552.6 %copy-start = (bf16[1024,640]{1,0:T(8,128)(2,1)S(1)}, bf16[1024,640]{1,0:T(8,128)(2,1)}, u32[]{:S(2)}) copy-start(bf16[1024,640]{1,0:T(8,128)(2,1)} %param.28) | copy-start | bytes 3932164
  7.2 305.3 %all-gather.4.cloned.1.call-start = ((), (), s32[]{:S(2)}) async-start(), calls=%async_computation | async-start | bytes 2113536 | tf_op jit(solution)/shard_map/all_gather | solution.py:66
  9.4 549.5 %all-reduce.8.cloned.1.call-start = ((), (), s32[]{:S(2)}) async-start(), calls=%async_computation.1 | async-start | bytes 6291456
  12.0 20.2 %copy-start.7 = (s32[512]{0:T(512)S(1)}, s32[512]{0:T(512)}, u32[]{:S(2)}) copy-start(s32[512]{0:T(512)} %param.21) | copy-start | bytes 6148
  12.0 23.9 %copy-start.12 = (bf16[512,512]{1,0:T(8,128)(2,1)S(1)}, bf16[512,512]{1,0:T(8,128)(2,1)}, u32[]{:S(2)}) copy-start(bf16[512,512]{1,0:T(8,128)(2,1)} %param.23) | copy-start | bytes 1572868
  32.2 4.2 copy-start.4
  32.2 4.7 copy-start.5
  389.0 8.2 %copy-start.1 = (f32[4,512,1536]{2,1,0:T(8,128)S(1)}, f32[4,512,1536]{2,1,0:T(8,128)}, u32[]{:S(2)}) copy-start(f32[4,512,1536]{2,1,0:T(8,128)} %get-tuple-element.20) | copy-start | bytes 37748740
  402.2 9.1 %copy-start.2 = (bf16[640,640]{1,0:T(8,128)(2,1)S(1)}, bf16[640,640]{1,0:T(8,128)(2,1)}, u32[]{:S(2)}) copy-start(bf16[640,640]{1,0:T(8,128)(2,1)} %param.30) | copy-start | bytes 2457604
  402.2 45.1 %copy-start.8 = (s32[4,64]{1,0:T(4,128)S(1)}, s32[4,64]{1,0:T(4,128)}, u32[]{:S(2)}) copy-start(s32[4,64]{1,0:T(4,128)} %param.18) | copy-start | bytes 3076
  402.2 49.2 %copy-start.9 = (s32[4]{0:T(128)S(1)}, s32[4]{0:T(128)}, u32[]{:S(2)}) copy-start(s32[4]{0:T(128)} %param.17) | copy-start | bytes 52
  402.2 157.6 %copy-start.3 = (bf16[512,1024]{1,0:T(8,128)(2,1)S(1)}, bf16[512,1024]{1,0:T(8,128)(2,1)}, u32[]{:S(2)}) copy-start(bf16[512,1024]{1,0:T(8,128)(2,1)} %param.27) | copy-start | bytes 3145732
  407.2 336.4 %all-reduce.10.cloned.1.call-start = ((), (), s32[]{:S(2)}) async-start(), calls=%async_computation.2 | async-start | bytes 294912
  446.8 0.5 copy-start.10
  598.9 6.0 copy-start.11
  605.0 51.6 %copy-start.6 = (s32[6144]{0:T(1024)S(1)}, s32[6144]{0:T(1024)}, u32[]{:S(2)}) copy-start(s32[6144]{0:T(1024)} %eq.42) | copy-start | bytes 73732
Sparse Core Ops, SparseCore 0:
  9.7 302.6 all-gather.3
  407.4 151.5 all-reduce.7
  666.3 77.2 all-reduce.9
where the time goes:
time: 753 us
  waiting for transfers between devices  394 us (52%)
  blocking collectives  240 us (32%)
  local copies, waits for them, and re-layouts  47.1 us (6%)
  matrix products  36.7 us (5%)
  other arithmetic  19.8 us (3%)
  between operations  14.7 us (2%)
    all_gather x1, waiting for transfers between devices, local(): asked = lax.all_gather(queries, ('phrase', 'vocab'), axis=0, tiled=True)  274 us
    unnamed x5, waiting for transfers between devices  120 us
    pmax x1, blocking collectives, local(): peak = lax.pmax(jnp.max(block_peak, -1), ('phrase', 'vocab'))  66.9 us
    unnamed x1, blocking collectives  63 us
    pmax x1, blocking collectives, local(): peak_rows = lax.pmax(jnp.max(logits, -1), 'vocab')  40.3 us
    all_gather x1, blocking collectives, local(): step_all = lax.all_gather(step_rows, 'vocab', axis=1, tiled=True)  35 us
    all_gather x1, blocking collectives, local(): joint_all = lax.all_gather(joint_rows, 'vocab', axis=0, tiled=True)  34.2 us
    gather x1, local copies, waits for them, and re-layouts, encode_local(): emb = phrase_table[ids]  20.2 us
  transfers between devices with their start and end apart: 3, of which 3 were waited for; matrix products, arithmetic and copies ran while one was open for 5% of the time, Pallas kernels for 0%

commit v1 on v0

v1 whole, which is shorter than its diff:
```python
import functools
import math

import jax
import jax.numpy as jnp
from jax import lax
from jax.experimental import pallas as pl
from jax.experimental.pallas import tpu as pltpu
from jax.sharding import Mesh, PartitionSpec as P

HEADS = 4
PAD = 16
AXES = ("y", "zl", "c", "x", "zh")
PHRASE = ("y", "zl", "c")
VOCAB = ("x", "zh")
PEERS = ("y", "zl", "x", "zh")
BF = jnp.bfloat16
F32 = jnp.float32
NT = (((1,), (1,)), ((), ()))


def mm(a, b):
    return jnp.dot(a, b, preferred_element_type=F32)


def encode_local(ids, lens, phrase_table, phrase_w):
    emb = phrase_table[ids]
    mask = (jnp.arange(ids.shape[1], dtype=jnp.int32)[None, :] < lens[:, None]).astype(BF)
    summed = jnp.einsum("npe,np->ne", emb, mask, preferred_element_type=F32)
    mean = (summed / lens[:, None].astype(F32)).astype(BF)
    return jnp.tanh(mm(mean, phrase_w)).astype(BF)


def attend_kernel(used, scale, q_ref, k_ref, v_ref, o_ref):
    rows, tile = q_ref.shape[0], 256
    k, v = k_ref[...], v_ref[...]
    for start in range(0, rows, tile):
        q = q_ref[start : start + tile, :]
        scores = lax.dot_general(q, k, NT, preferred_element_type=F32) * scale
        peak = jnp.max(scores, -1, keepdims=True)
        weights = jnp.exp(scores - peak)
        total = jnp.sum(weights, -1, keepdims=True)
        part = mm(weights.astype(BF), v) / total
        rest = peak + jnp.log(total)
        groups = tile // PAD
        shape = (groups, PAD, part.shape[1])
        row = lax.broadcasted_iota(jnp.int32, shape, 1)
        lane = lax.broadcasted_iota(jnp.int32, shape, 2)
        part = part.reshape(shape)
        for piece in range(3):
            sent = rest.astype(BF).astype(F32)
            rest = rest - sent
            spread = jnp.broadcast_to(sent, (tile, shape[2])).reshape(shape)
            line = jnp.sum(jnp.where(lane == row, spread, 0.0), 1, keepdims=True)
            part = jnp.where(row == used + piece, line, part)
        o_ref[start : start + tile, :] = part.reshape(tile, shape[2]).astype(BF)


def attend(asked, keys, values, used):
    rows, width = asked.shape
    head = width // HEADS
    phrases = keys.shape[0]
    return pl.pallas_call(
        functools.partial(attend_kernel, used, 1.0 / math.sqrt(head)),
        grid=(HEADS,),
        in_specs=[
            pl.BlockSpec((rows, head), lambda h: (0, h)),
            pl.BlockSpec((phrases, head), lambda h: (0, h)),
            pl.BlockSpec((phrases, head), lambda h: (0, h)),
        ],
        out_specs=pl.BlockSpec((rows, head), lambda h: (0, h)),
        out_shape=jax.ShapeDtypeStruct((rows, width), BF),
        cost_estimate=pl.CostEstimate(
            flops=4 * rows * phrases * width,
            bytes_accessed=4 * rows * width + 4 * phrases * width,
            transcendentals=rows * phrases * HEADS,
        ),
    )(asked, keys, values)


def join_kernel(used, parts_ref, frames_ref, context_w_ref, joint_w_ref, o_ref):
    peers, pad, width = parts_ref.shape
    head = width // HEADS
    row = lax.broadcasted_iota(jnp.int32, (peers, pad, head), 1)
    lane = lax.broadcasted_iota(jnp.int32, (peers, pad, head), 2)
    columns = []
    for h in range(HEADS):
        block = parts_ref[:, :, h * head : (h + 1) * head].astype(F32)
        lse = jnp.sum(jnp.where((row >= used) & (row < used + 3), block, 0.0), 1, keepdims=True)
        factor = jnp.exp(lse - jnp.max(lse, 0, keepdims=True))
        factor = factor / jnp.sum(factor, 0, keepdims=True)
        weight = jnp.sum(jnp.where(lane == row, factor, 0.0), -1, keepdims=True)
        columns.append(jnp.sum(weight * block, 0))
    context = jnp.concatenate(columns, 1).astype(BF)
    biased = (frames_ref[...].astype(F32) + mm(context, context_w_ref[...])).astype(BF)
    o_ref[...] = mm(biased, joint_w_ref[...]).astype(BF)


def join(parts, frames, context_w, joint_w, used):
    return pl.pallas_call(
        functools.partial(join_kernel, used),
        out_shape=jax.ShapeDtypeStruct((frames.shape[0], joint_w.shape[1]), BF),
    )(parts, frames, context_w, joint_w)


def joint_kernel(used, first_ref, enc_ref, pred_ref, out_w_ref, labels_ref, o_ref, enc_s, in_s):
    groups, pad, width = enc_ref.shape
    frames = groups * used
    own = pred_ref.shape[0]
    cols = out_w_ref.shape[0]
    tile = 256

    @pl.when(pl.program_id(0) == 0)
    def _():
        for g in range(groups):
            enc_s[g * used : (g + 1) * used, :] = enc_ref[g, :used, :].astype(F32)

    for u in range(own):
        in_s[u * frames : (u + 1) * frames, :] = jnp.tanh(
            enc_s[...] + pred_ref[u : u + 1, :]
        ).astype(BF)
    column = lax.broadcasted_iota(jnp.int32, (cols, tile), 0) + first_ref[0]
    lines = tile // 128
    stat = o_ref.shape[1] // 3
    for start in range(0, own * frames, tile):
        logits = lax.dot_general(
            out_w_ref[...], in_s[start : start + tile, :], NT, preferred_element_type=F32
        )
        peak = jnp.max(logits, 0, keepdims=True)
        total = jnp.sum(jnp.exp(logits - peak), 0, keepdims=True)
        lse = peak + jnp.log(total)
        label = jnp.sum(jnp.where(column == labels_ref[0, :, start : start + tile], logits, 0.0), 0, keepdims=True)
        for i in range(lines):
            at = start // 128 + i
            piece = slice(i * 128, (i + 1) * 128)
            o_ref[0, at : at + 1, :] = lse[:, piece]
            o_ref[0, stat + at : stat + at + 1, :] = label[:, piece]
            o_ref[0, 2 * stat + at : 2 * stat + at + 1, :] = logits[0:1, piece]


def joint(enc_all, pred, out_wt, labels, first, used, n_vocab):
    groups, pad, width = enc_all.shape
    frames = groups * used
    positions = pred.shape[0]
    own = positions // n_vocab
    cols = out_wt.shape[0]
    pairs = own * frames
    stat = 8
    spread = jnp.broadcast_to(labels.reshape(n_vocab, 1, own, 1), (n_vocab, 1, own, frames))
    return pl.pallas_call(
        functools.partial(joint_kernel, used),
        grid=(n_vocab,),
        in_specs=[
            pl.BlockSpec(memory_space=pltpu.SMEM),
            pl.BlockSpec((groups, pad, width), lambda i: (0, 0, 0)),
            pl.BlockSpec((own, width), lambda i: (i, 0)),
            pl.BlockSpec((cols, width), lambda i: (0, 0)),
            pl.BlockSpec((1, 1, pairs), lambda i: (i, 0, 0)),
        ],
        out_specs=pl.BlockSpec((1, 3 * stat, 128), lambda i: (i, 0, 0)),
        out_shape=jax.ShapeDtypeStruct((n_vocab, 3 * stat, 128), F32),
        scratch_shapes=[pltpu.VMEM((frames, width), F32), pltpu.VMEM((pairs, width), BF)],
        cost_estimate=pl.CostEstimate(
            flops=2 * n_vocab * pairs * width * cols,
            bytes_accessed=2 * cols * width,
            transcendentals=n_vocab * pairs * (width + cols),
        ),
    )(first, enc_all, pred, out_wt, spread.reshape(n_vocab, 1, pairs))


def local(
    frames,
    frame_lens,
    labels,
    label_lens,
    phrase_ids,
    phrase_lens,
    phrase_table,
    phrase_w,
    key_w,
    value_w,
    query_w,
    context_w,
    joint_enc_w,
    pred_table,
    pred_w,
    out_w,
):
    n_vocab = lax.axis_size(VOCAB)
    n_phrase = lax.axis_size(PHRASE)
    n_peers = lax.axis_size(PEERS)
    used = frames.shape[0]
    frames_pad = jnp.pad(frames, ((0, PAD - used), (0, 0)))
    queries = mm(frames_pad, query_w).astype(BF)
    asked = lax.all_to_all(
        jnp.broadcast_to(queries[None], (n_peers,) + queries.shape), PEERS, 0, 0, tiled=True
    )

    phrase_vec = encode_local(phrase_ids, phrase_lens, phrase_table, phrase_w)
    other_vec = lax.ppermute(phrase_vec, "c", [(0, 1), (1, 0)])
    vecs = jnp.concatenate([phrase_vec, other_vec], 0)
    keys = mm(vecs, key_w).astype(BF)
    values = mm(vecs, value_w).astype(BF)

    utts, positions = labels.shape
    frames_dev = used * n_vocab
    tlen = frames_dev * n_phrase // utts
    start = lax.axis_index(PHRASE) * frames_dev
    utt = start // tlen
    own_labels = lax.dynamic_slice_in_dim(labels, utt, 1, 0)[0]
    picked = jnp.concatenate([jnp.zeros((1,), jnp.int32), own_labels[:-1]])
    predictor = mm(pred_table[picked], pred_w).astype(BF).astype(F32)
    out_wt = out_w.T

    parts = attend(asked.reshape(n_peers * PAD, -1), keys, values, used)
    parts = lax.all_to_all(parts.reshape(n_peers, PAD, -1), PEERS, 0, 0, tiled=True)
    enc = join(parts, frames_pad, context_w, joint_enc_w, used)
    enc_all = lax.all_to_all(
        jnp.broadcast_to(enc[None], (n_vocab,) + enc.shape), VOCAB, 0, 0, tiled=True
    )
    vocab_index = lax.axis_index(VOCAB)
    cols = out_w.shape[1]
    first = (vocab_index * cols).astype(jnp.int32).reshape(1)
    stats = joint(enc_all, predictor, out_wt, own_labels, first, used, n_vocab)
    stats = lax.all_to_all(stats, VOCAB, 0, 0, tiled=True)

    own = positions // n_vocab
    pairs = own * frames_dev
    stats = stats.reshape(n_vocab, 3, -1)[:, :, :pairs]
    lse, label, blank = stats[:, 0], stats[:, 1], stats[0, 2]
    peak = jnp.max(lse, 0)
    norm = peak + jnp.log(jnp.sum(jnp.exp(lse - peak), 0))
    label = jnp.sum(label, 0)
    moment = start % tlen + jnp.arange(frames_dev, dtype=jnp.int32)
    position = vocab_index * own + jnp.arange(own, dtype=jnp.int32)
    frame_len = lax.dynamic_slice_in_dim(frame_lens, utt, 1, 0)
    label_len = lax.dynamic_slice_in_dim(label_lens, utt, 1, 0)
    live = (moment < frame_len)[None, :]
    blank = (blank - norm).reshape(own, frames_dev)
    label = (label - norm).reshape(own, frames_dev)
    blank_out = jnp.where(live & (position <= label_len)[:, None], blank, 0.0)
    label_out = jnp.where(live & (position < label_len)[:, None], label, 0.0)
    return (blank_out.T, label_out.T)


def solution(mesh):
    n_phrase, n_vocab = mesh.devices.shape
    fine = Mesh(mesh.devices.reshape(n_phrase // 4, 2, 2, n_vocab // 2, 2), AXES)
    rows = P(AXES, None)
    in_specs = (
        rows,
        P(),
        P(),
        P(),
        rows,
        P(AXES),
        P(),
        P(),
        P(),
        P(),
        P(),
        P(),
        P(),
        P(),
        P(),
        P(None, VOCAB),
    )
    out_specs = (P(PHRASE, VOCAB), P(PHRASE, VOCAB))
    return jax.shard_map(local, mesh=fine, in_specs=in_specs, out_specs=out_specs, check_vma=False)
```

time: 753 us -> 141 us (0.19)
  waiting for transfers between devices: 394 us -> 34.4 us
  blocking collectives: 240 us -> 0 us
  Pallas kernels: 0 us -> 27 us
  matrix products: 36.7 us -> 11.7 us
  starting transfers between devices: 0.3 us -> 25.1 us
  other arithmetic: 19.8 us -> 4.44 us
  between operations: 14.7 us -> 0.84 us
  local copies, waits for them, and re-layouts: 47.1 us -> 36.5 us
    all_gather x1 -> x0, waiting for transfers between devices: 274 us -> none  [local(): asked = lax.all_gather(queries, ('phrase', 'vocab'), axis=0, tiled=True)]
    unnamed x5 -> x0, waiting for transfers between devices: 120 us -> none
    pmax x2 -> x0, blocking collectives: 107 us -> none  [the longest x1 66.9 us: local(): peak = lax.pmax(jnp.max(block_peak, -1), ('phrase', 'vocab'))]
    all_gather x2 -> x0, blocking collectives: 69.3 us -> none  [the longest x1 35 us: local(): step_all = lax.all_gather(step_rows, 'vocab', axis=1, tiled=True)]
    unnamed x1 -> x0, blocking collectives: 63 us -> none
    all_to_all x0 -> x4, waiting for transfers between devices: none -> 34.4 us  [the longest x1 13.6 us: local(): lax.all_to_all(jnp.broadcast_to(queries[None], (n_peers,) + queries.shape...]
    pallas_call x0 -> x3, Pallas kernels: none -> 27 us  [the longest x1 12 us: attend(): pl.pallas_call(functools.partial(attend_kernel, used, 1.0 / math.sqrt(hea...]
    all_to_all x0 -> x4, starting transfers between devices: none -> 25.1 us  [the longest x1 11.5 us: local(): lax.all_to_all(jnp.broadcast_to(queries[None], (n_peers,) + queries.shape...]
  transfers between devices with their start and end apart: 3 -> 5, of which waited for: 3 -> 4; matrix products, arithmetic and copies ran while one was open for 5% -> 14% of each run, Pallas kernels for 0% -> 0%
where the time goes in v1:
time: 141 us; the launch traced here: 140 us
  local copies, waits for them, and re-layouts  36.5 us (26%)
  waiting for transfers between devices  34.4 us (24%)
  Pallas kernels  27 us (19%)
  starting transfers between devices  25.1 us (18%)
  matrix products  11.7 us (8%)
  other arithmetic  4.44 us (3%)
    gather x1, local copies, waits for them, and re-layouts, encode_local(): emb = phrase_table[ids]  20.2 us
    all_to_all x1, waiting for transfers between devices, local(): lax.all_to_all(jnp.broadcast_to(queries[None], (n_peers,) + queries.shape...  13.6 us
    pallas_call x1, Pallas kernels, attend(): pl.pallas_call(functools.partial(attend_kernel, used, 1.0 / math.sqrt(hea...  12 us
    all_to_all x1, starting transfers between devices, local(): lax.all_to_all(jnp.broadcast_to(queries[None], (n_peers,) + queries.shape...  11.5 us
    all_to_all x1, waiting for transfers between devices, local(): lax.all_to_all(parts.reshape(n_peers, PAD, -1), PEERS, 0, 0, tiled=True)  11.4 us
    pallas_call x1, Pallas kernels, joint(): pl.pallas_call(functools.partial(joint_kernel, used), grid=(n_vocab,), in...  11.1 us
    dot_general x5, matrix products, mm(): return jnp.dot(a, b, preferred_element_type=F32)  8.27 us
    all_to_all x1, waiting for transfers between devices, local(): stats = lax.all_to_all(stats, VOCAB, 0, 0, tiled=True)  7.15 us
  transfers between devices with their start and end apart: 5, of which 4 were waited for; matrix products, arithmetic and copies ran while one was open for 14% of the time, Pallas kernels for 0%

profile of v1, /device:TPU:0, one launch (start us, length us, event | category | flops | bytes accessed | tf_op | source)
XLA Modules:
  0.0 140.0 jit_solution(14625250813678111205)
XLA Ops:
  0.6 0.9 fusion.8
  1.6 0.7 convert_element_type.29
  2.2 0.7 compare_select_fusion
  3.3 20.2 %gather_fusion = bf16[4096,512]{1,0:T(8,128)(2,1)} fusion(bf16[4096,512]{1,0:T(8,128)(2,1)} %param.22, s32[4096]{0:T(1024)S(1)} %broadcast_clamp_fusion), kind=kCustom, calls=%fused_computation | custom fusion | bytes 8404992 | tf_op jit(solution)/shard_map/gather | solution.py:27
  23.4 3.5 %fusion = f32[512,1,512]{2,1,0:T(1,128)S(1)} fusion(bf16[4096,512]{1,0:T(8,128)(2,1)} %gather_fusion, pred[512,8,1]{1,0,2:T(32,128)(4,1)S(1)} %fusion.8), kind=kOutput, calls=%fused_computation.2 | convolution fusion | flops 4194304 | bytes 5246976 | tf_op jit(solution)/shard_map/npe,np->ne/dot_general | solution.py:29
  26.9 1.3 fusion.2
  28.5 1.1 broadcast_in_dim.16
  29.6 11.5 %all-to-all-start = ((bf16[64,16,512]{2,1,0:T(8,128)(2,1)}), bf16[64,16,512]{2,1,0:T(8,128)(2,1)S(1)}, u32[]{:S(2)}, u32[]{:S(2)}) async-start(bf16[64,16,512]{2,1,0:T(8,128)(2,1)} %broadcast_in_dim.16), calls=%async_computation | async-start | bytes 2097152 | tf_op jit(solution)/shard_map/all_to_all | solution.py:195
  41.1 2.9 %convolution_convert_fusion.v_ref = bf16[1024,512]{1,0:T(8,128)(2,1)} fusion(bf16[512,512]{1,0:T(8,128)(2,1)S(1)} %copy-done.7, bf16[512,512]{1,0:T(8,128)(2,1)} %collective-permute-done, bf16[512,512]{1,0:T(8,128)(2,1)} %fusion.2), kind=kOutput, calls=%fused_computation.4 | convolution fusion | flops 539492352 | bytes 2621440 | tf_op jit(solution)/shard_map/dot_general | solution.py:23
  44.1 2.9 %convolution_convert_fusion.1.k_ref = bf16[1024,512]{1,0:T(8,128)(2,1)} fusion(bf16[512,512]{1,0:T(8,128)(2,1)S(1)} %copy-done.8, bf16[512,512]{1,0:T(8,128)(2,1)} %collective-permute-done, bf16[512,512]{1,0:T(8,128)(2,1)} %fusion.2), kind=kOutput, calls=%fused_computation.5 | convolution fusion | flops 539492352 | bytes 2621440 | tf_op jit(solution)/shard_map/dot_general | solution.py:23
  46.9 13.6 %all-to-all-done = bf16[64,16,512]{2,1,0:T(8,128)(2,1)S(1)} async-done(((bf16[64,16,512]{2,1,0:T(8,128)(2,1)}), bf16[64,16,512]{2,1,0:T(8,128)(2,1)S(1)}, u32[]{:S(2)}, u32[]{:S(2)}) %all-to-all-start) | async-done | bytes 1048608 | tf_op jit(solution)/shard_map/all_to_all | solution.py:195
  60.6 1.0 copy-done.2
  61.6 12.0 %shard_map.167 = bf16[1024,512]{1,0:T(8,128)(2,1)} custom-call(bf16[1024,512]{1,0:T(8,128)(2,1)} %bitcast.37, bf16[1024,512]{1,0:T(8,128)(2,1)} %convolution_convert_fusion.1.k_ref, bf16[1024,512]{1,0:T(8,128)(2,1)} %convolution_convert_fusion.v_ref), custom_call_target="tpu_custom_call" | custom-call | flops 2147483648 | bytes 4194304 | tf_op jit(solution)/shard_map/pallas_call | solution.py:63
  73.6 5.2 %all-to-all-start.1 = ((bf16[64,16,512]{2,1,0:T(8,128)(2,1)}), bf16[64,16,512]{2,1,0:T(8,128)(2,1)S(1)}, u32[]{:S(2)}, u32[]{:S(2)}) async-start(bf16[64,16,512]{2,1,0:T(8,128)(2,1)} %bitcast.36), calls=%async_computation.1 | async-start | bytes 2097152 | tf_op jit(solution)/shard_map/all_to_all | solution.py:216
  79.9 1.3 fusion.17
  81.4 3.9 %gather_fusion.1 = bf16[64,640]{1,0:T(8,128)(2,1)S(1)} fusion(bf16[4096,640]{1,0:T(8,128)(2,1)} %param.29, s32[1024]{0:T(1024)S(1)} %pad_clamp_fusion), kind=kCustom, calls=%fused_computation.1 | custom fusion | bytes 164096 | tf_op jit(solution)/shard_map/gather | solution.py:212
  85.3 11.4 %all-to-all-done.1.parts_ref = bf16[64,16,512]{2,1,0:T(8,128)(2,1)S(1)} async-done(((bf16[64,16,512]{2,1,0:T(8,128)(2,1)}), bf16[64,16,512]{2,1,0:T(8,128)(2,1)S(1)}, u32[]{:S(2)}, u32[]{:S(2)}) %all-to-all-start.1) | async-done | bytes 1048608 | tf_op jit(solution)/shard_map/all_to_all | solution.py:216
  96.7 1.0 copy-done.1
  97.6 4.0 %shard_map.168 = bf16[16,640]{1,0:T(8,128)(2,1)} custom-call(bf16[64,16,512]{2,1,0:T(8,128)(2,1)} %copy-done.1, bf16[16,1024]{1,0:T(8,128)(2,1)} %pad.4.frames_ref, bf16[512,1024]{1,0:T(8,128)(2,1)} %context_w_ref.1, bf16[1024,640]{1,0:T(8,128)(2,1)} %joint_w_ref.1), custom_call_target="tpu_custom_call" | custom-call | tf_op jit(solution)/shard_map/pallas_call | solution.py:100
  101.6 1.4 %broadcast_in_dim.18 = bf16[8,16,640]{2,1,0:T(8,128)(2,1)} broadcast(bf16[16,640]{1,0:T(8,128)(2,1)} %shard_map.168), dimensions={1,2} | broadcast | bytes 184320 | tf_op jit(solution)/shard_map/broadcast_in_dim | solution.py:219
  103.0 3.4 %all-to-all-start.2 = ((bf16[8,16,640]{2,1,0:T(8,128)(2,1)}), bf16[8,16,640]{2,1,0:T(8,128)(2,1)S(1)}, u32[]{:S(2)}, u32[]{:S(2)}) async-start(bf16[8,16,640]{2,1,0:T(8,128)(2,1)} %broadcast_in_dim.18), calls=%async_computation.2 | async-start | bytes 327680 | tf_op jit(solution)/shard_map/all_to_all | solution.py:218
  106.4 0.9 fusion.3.pred_ref
  107.5 0.7 broadcast_in_dim.42.labels_ref
  108.2 2.2 %copy.20 = bf16[640,512]{0,1:T(8,128)(2,1)} copy(bf16[640,512]{1,0:T(8,128)(2,1)} %param.31) | data formatting | bytes 1310720 | tf_op args[15]
  111.0 0.6 dynamic_slice.10
  112.3 2.2 %all-to-all-done.2.enc_ref = bf16[8,16,640]{2,1,0:T(8,128)(2,1)S(1)} async-done(((bf16[8,16,640]{2,1,0:T(8,128)(2,1)}), bf16[8,16,640]{2,1,0:T(8,128)(2,1)S(1)}, u32[]{:S(2)}, u32[]{:S(2)}) %all-to-all-start.2) | async-done | bytes 163872 | tf_op jit(solution)/shard_map/all_to_all | solution.py:218
  114.4 0.7 copy-done.4
  115.1 11.1 %shard_map.169 = f32[8,24,128]{2,1,0:T(8,128)} custom-call(s32[1]{0:T(128)} %bitcast.2.first_ref, bf16[8,16,640]{2,1,0:T(8,128)(2,1)} %copy-done.4, f32[64,640]{1,0:T(8,128)} %fusion.3.pred_ref, bf16[512,640]{1,0:T(8,128)(2,1)} %bitcast.38, s32[8,1,768]{2,1,0:T(1,128)} %broadcast_in_dim.42.labels_ref), custom_call_target="tpu_custom_call" | custom-call | flops 4026531840 | bytes 655360 | tf_op jit(solution)/shard_map/pallas_call | solution.py:150
  126.2 5.0 %all-to-all-start.3 = ((f32[8,24,128]{2,1,0:T(8,128)}), f32[8,24,128]{2,1,0:T(8,128)S(1)}, u32[]{:S(2)}, u32[]{:S(2)}) async-start(f32[8,24,128]{2,1,0:T(8,128)} %shard_map.169), calls=%async_computation.3 | async-start | bytes 196608 | tf_op jit(solution)/shard_map/all_to_all | solution.py:225
  131.1 0.7 add_compare_fusion
  131.8 7.2 %all-to-all-done.3 = f32[8,24,128]{2,1,0:T(8,128)S(1)} async-done(((f32[8,24,128]{2,1,0:T(8,128)}), f32[8,24,128]{2,1,0:T(8,128)S(1)}, u32[]{:S(2)}, u32[]{:S(2)}) %all-to-all-start.3) | async-done | bytes 98336 | tf_op jit(solution)/shard_map/all_to_all | solution.py:225
  139.3 0.7 select_bitcast_fusion
  (42 shorter events, 3.5 us)
Async XLA Ops:
  0.6 27.6 %copy-start = (bf16[1024,512]{1,0:T(8,128)(2,1)S(1)}, bf16[1024,512]{1,0:T(8,128)(2,1)}, u32[]{:S(2)}) copy-start(bf16[1024,512]{1,0:T(8,128)(2,1)} %param.26) | copy-start | bytes 3145732
  23.4 3.5 %copy-start.6 = (bf16[512,512]{1,0:T(8,128)(2,1)S(1)}, bf16[512,512]{1,0:T(8,128)(2,1)}, u32[]{:S(2)}) copy-start(bf16[512,512]{1,0:T(8,128)(2,1)} %param.23) | copy-start | bytes 1572868
  23.4 4.8 %copy-start.5 = (bf16[12,1024]{1,0:T(8,128)(2,1)S(1)}, bf16[12,1024]{1,0:T(8,128)(2,1)}, u32[]{:S(2)}) copy-start(bf16[12,1024]{1,0:T(8,128)(2,1)} %param.16) | copy-start | bytes 73732
  26.9 14.2 %copy-start.7 = (bf16[512,512]{1,0:T(8,128)(2,1)S(1)}, bf16[512,512]{1,0:T(8,128)(2,1)}, u32[]{:S(2)}) copy-start(bf16[512,512]{1,0:T(8,128)(2,1)} %param.25) | copy-start | bytes 1572868
  28.2 15.8 %copy-start.8 = (bf16[512,512]{1,0:T(8,128)(2,1)S(1)}, bf16[512,512]{1,0:T(8,128)(2,1)}, u32[]{:S(2)}) copy-start(bf16[512,512]{1,0:T(8,128)(2,1)} %param.24) | copy-start | bytes 1572868
  28.2 12.9 %collective-permute-start = (bf16[512,512]{1,0:T(8,128)(2,1)}, bf16[512,512]{1,0:T(8,128)(2,1)}, u32[]{:S(2)}, u32[]{:S(2)}) collective-permute-start(bf16[512,512]{1,0:T(8,128)(2,1)} %fusion.2), channel_id=1, source_target_pairs={{0,8},{8,0},{1,9},{9,1},{2,10},{10,2},{3,11},{11,3},{4,12},{12,4},... | collective-permute-start | bytes 1572872 | tf_op jit(solution)/shard_map/ppermute | solution.py:200
  29.6 31.0 %all-to-all-start = ((bf16[64,16,512]{2,1,0:T(8,128)(2,1)}), bf16[64,16,512]{2,1,0:T(8,128)(2,1)S(1)}, u32[]{:S(2)}, u32[]{:S(2)}) async-start(bf16[64,16,512]{2,1,0:T(8,128)(2,1)} %broadcast_in_dim.16), calls=%async_computation | async-start | bytes 2097152 | tf_op jit(solution)/shard_map/all_to_all | solution.py:195
  60.6 1.0 copy-start.2
  73.5 32.9 %copy-start.3 = (bf16[640,640]{1,0:T(8,128)(2,1)S(1)}, bf16[640,640]{1,0:T(8,128)(2,1)}, u32[]{:S(2)}) copy-start(bf16[640,640]{1,0:T(8,128)(2,1)} %param.30) | copy-start | bytes 2457604
  73.5 36.8 %copy-start.9 = (s32[4]{0:T(128)S(1)}, s32[4]{0:T(128)}, u32[]{:S(2)}) copy-start(s32[4]{0:T(128)} %param.17) | copy-start | bytes 52
  73.6 37.4 %copy-start.10 = (s32[4]{0:T(128)S(1)}, s32[4]{0:T(128)}, u32[]{:S(2)}) copy-start(s32[4]{0:T(128)} %param.19) | copy-start | bytes 52
  73.6 23.1 %all-to-all-start.1 = ((bf16[64,16,512]{2,1,0:T(8,128)(2,1)}), bf16[64,16,512]{2,1,0:T(8,128)(2,1)S(1)}, u32[]{:S(2)}, u32[]{:S(2)}) async-start(bf16[64,16,512]{2,1,0:T(8,128)(2,1)} %bitcast.36), calls=%async_computation.1 | async-start | bytes 2097152 | tf_op jit(solution)/shard_map/all_to_all | solution.py:216
  96.7 1.0 copy-start.1
  103.0 11.4 %all-to-all-start.2 = ((bf16[8,16,640]{2,1,0:T(8,128)(2,1)}), bf16[8,16,640]{2,1,0:T(8,128)(2,1)S(1)}, u32[]{:S(2)}, u32[]{:S(2)}) async-start(bf16[8,16,640]{2,1,0:T(8,128)(2,1)} %broadcast_in_dim.18), calls=%async_computation.2 | async-start | bytes 327680 | tf_op jit(solution)/shard_map/all_to_all | solution.py:218
  114.4 0.7 copy-start.4
  126.2 12.8 %all-to-all-start.3 = ((f32[8,24,128]{2,1,0:T(8,128)}), f32[8,24,128]{2,1,0:T(8,128)S(1)}, u32[]{:S(2)}, u32[]{:S(2)}) async-start(f32[8,24,128]{2,1,0:T(8,128)} %shard_map.169), calls=%async_computation.3 | async-start | bytes 196608 | tf_op jit(solution)/shard_map/all_to_all | solution.py:225

commit v2 on v1

--- a/solution.py
+++ b/solution.py
@@ -16,6 +16,7 @@
 PEERS = ("y", "zl", "x", "zh")
 BF = jnp.bfloat16
 F32 = jnp.float32
+LOG2E = 1.0 / math.log(2.0)
 NT = (((1,), (1,)), ((), ()))
 
 
@@ -23,25 +24,74 @@
     return jnp.dot(a, b, preferred_element_type=F32)
 
 
-def encode_local(ids, lens, phrase_table, phrase_w):
-    emb = phrase_table[ids]
-    mask = (jnp.arange(ids.shape[1], dtype=jnp.int32)[None, :] < lens[:, None]).astype(BF)
-    summed = jnp.einsum("npe,np->ne", emb, mask, preferred_element_type=F32)
-    mean = (summed / lens[:, None].astype(F32)).astype(BF)
-    return jnp.tanh(mm(mean, phrase_w)).astype(BF)
+def encode_kernel(ids_ref, lens_ref, table_ref, phrase_w_ref, key_w_ref, value_w_ref, k_ref, v_ref):
+    rows, tokens = ids_ref.shape
+    vocab = table_ref.shape[0]
+    lens = lens_ref[...]
+    slot = lax.broadcasted_iota(jnp.int32, (rows, tokens), 1)
+    ids = jnp.where(slot < lens, ids_ref[...], -1)
+    lane = lax.broadcasted_iota(jnp.int32, (rows, 128), 1)
+    blocks, units = [], []
+    for t in range(tokens):
+        token = jnp.broadcast_to(ids[:, t : t + 1], (rows, 128))
+        blocks.append(lax.shift_right_arithmetic(token, 7).astype(F32).astype(BF))
+        units.append(jnp.where((token & 127) == lane, 1.0, 0.0).astype(BF))
+    zero = jnp.zeros((rows, 128), BF)
+    summed = jnp.zeros((rows, table_ref.shape[1]), F32)
+    for pair in range(vocab // 256):
+        counts = []
+        for block in (2 * pair, 2 * pair + 1):
+            count = zero
+            for t in range(tokens):
+                count += jnp.where(blocks[t] == BF(block), units[t], zero)
+            counts.append(count)
+        summed += mm(jnp.concatenate(counts, 1), table_ref[pair * 256 : (pair + 1) * 256, :])
+    mean = (summed / lens.astype(F32)).astype(BF)
+    vec = jnp.tanh(mm(mean, phrase_w_ref[...])).astype(BF)
+    k_ref[...] = mm(vec, key_w_ref[...]).astype(BF)
+    v_ref[...] = mm(vec, value_w_ref[...]).astype(BF)
+
+
+def encode(ids, lens, table, phrase_w, key_w, value_w):
+    phrases, tokens = ids.shape
+    vocab, width = table.shape
+    tile = 256
+    whole = lambda a: pl.BlockSpec(a.shape, lambda i: (0, 0))
+    return pl.pallas_call(
+        encode_kernel,
+        grid=(phrases // tile,),
+        in_specs=[
+            pl.BlockSpec((tile, tokens), lambda i: (i, 0)),
+            pl.BlockSpec((tile, 1), lambda i: (i, 0)),
+            whole(table),
+            whole(phrase_w),
+            whole(key_w),
+            whole(value_w),
+        ],
+        out_specs=[pl.BlockSpec((tile, width), lambda i: (i, 0))] * 2,
+        out_shape=[jax.ShapeDtypeStruct((phrases, width), BF)] * 2,
+        cost_estimate=pl.CostEstimate(
+            flops=40 * phrases * vocab * width,
+            bytes_accessed=2 * vocab * width,
+            transcendentals=phrases * width,
+        ),
+    )(ids, lens.reshape(-1, 1), table, phrase_w, key_w, value_w)
 
 
 def attend_kernel(used, scale, q_ref, k_ref, v_ref, o_ref):
     rows, tile = q_ref.shape[0], 256
     k, v = k_ref[...], v_ref[...]
+    head = v.shape[1]
+    v_ones = jnp.concatenate([v, jnp.ones_like(v)], 1)
     for start in range(0, rows, tile):
         q = q_ref[start : start + tile, :]
-        scores = lax.dot_general(q, k, NT, preferred_element_type=F32) * scale
+        scores = lax.dot_general(q, k, NT, preferred_element_type=F32)
         peak = jnp.max(scores, -1, keepdims=True)
-        weights = jnp.exp(scores - peak)
-        total = jnp.sum(weights, -1, keepdims=True)
-        part = mm(weights.astype(BF), v) / total
-        rest = peak + jnp.log(total)
+        weights = jnp.exp2((scores - peak) * (scale * LOG2E)).astype(BF)
+        sums = mm(weights, v_ones)
+        total = sums[:, head:]
+        part = sums[:, :head] / total
+        rest = peak * scale + jnp.log(total)
         groups = tile // PAD
         shape = (groups, PAD, part.shape[1])
         row = lax.broadcasted_iota(jnp.int32, shape, 1)
@@ -50,8 +100,7 @@
         for piece in range(3):
             sent = rest.astype(BF).astype(F32)
             rest = rest - sent
-            spread = jnp.broadcast_to(sent, (tile, shape[2])).reshape(shape)
-            line = jnp.sum(jnp.where(lane == row, spread, 0.0), 1, keepdims=True)
+            line = jnp.sum(jnp.where(lane == row, sent.reshape(shape), 0.0), 1, keepdims=True)
             part = jnp.where(row == used + piece, line, part)
         o_ref[start : start + tile, :] = part.reshape(tile, shape[2]).astype(BF)
 
@@ -93,17 +142,19 @@
         columns.append(jnp.sum(weight * block, 0))
     context = jnp.concatenate(columns, 1).astype(BF)
     biased = (frames_ref[...].astype(F32) + mm(context, context_w_ref[...])).astype(BF)
-    o_ref[...] = mm(biased, joint_w_ref[...]).astype(BF)
-
-
-def join(parts, frames, context_w, joint_w, used):
+    joint_rows = mm(biased, joint_w_ref[...]).astype(BF)
+    for i in range(o_ref.shape[0]):
+        o_ref[i] = joint_rows
+
+
+def join(parts, frames, context_w, joint_w, used, copies):
     return pl.pallas_call(
         functools.partial(join_kernel, used),
-        out_shape=jax.ShapeDtypeStruct((frames.shape[0], joint_w.shape[1]), BF),
+        out_shape=jax.ShapeDtypeStruct((copies, frames.shape[0], joint_w.shape[1]), BF),
     )(parts, frames, context_w, joint_w)
 
 
-def joint_kernel(used, first_ref, enc_ref, pred_ref, out_w_ref, labels_ref, o_ref, enc_s, in_s):
+def joint_kernel(used, enc_ref, pred_ref, out_w_ref, label_w_ref, o_ref, enc_s, w_s):
     groups, pad, width = enc_ref.shape
     frames = groups * used
     own = pred_ref.shape[0]
@@ -114,23 +165,29 @@
     def _():
         for g in range(groups):
             enc_s[g * used : (g + 1) * used, :] = enc_ref[g, :used, :].astype(F32)
-
-    for u in range(own):
-        in_s[u * frames : (u + 1) * frames, :] = jnp.tanh(
-            enc_s[...] + pred_ref[u : u + 1, :]
-        ).astype(BF)
-    column = lax.broadcasted_iota(jnp.int32, (cols, tile), 0) + first_ref[0]
-    lines = tile // 128
+        w_s[:cols, :] = out_w_ref[...]
+
+    w_s[cols:, :] = label_w_ref[0]
+    pred = pred_ref[...]
     stat = o_ref.shape[1] // 3
     for start in range(0, own * frames, tile):
-        logits = lax.dot_general(
-            out_w_ref[...], in_s[start : start + tile, :], NT, preferred_element_type=F32
-        )
+        pieces, at = [], start
+        while at < start + tile:
+            u, f = at // frames, at % frames
+            size = min(frames - f, start + tile - at)
+            pieces.append(jnp.tanh(enc_s[f : f + size, :] + pred[u : u + 1, :]).astype(BF))
+            at += size
+        rows = jnp.concatenate(pieces, 0)
+        found = lax.dot_general(w_s[...], rows, NT, preferred_element_type=F32)
+        logits = found[:cols]
         peak = jnp.max(logits, 0, keepdims=True)
-        total = jnp.sum(jnp.exp(logits - peak), 0, keepdims=True)
+        total = jnp.sum(jnp.exp2((logits - peak) * LOG2E), 0, keepdims=True)
         lse = peak + jnp.log(total)
-        label = jnp.sum(jnp.where(column == labels_ref[0, :, start : start + tile], logits, 0.0), 0, keepdims=True)
-        for i in range(lines):
+        pair = lax.broadcasted_iota(jnp.int32, (own, tile), 1) + start
+        low = lax.broadcasted_iota(jnp.int32, (own, tile), 0) * frames
+        mine = (pair >= low) & (pair < low + frames)
+        label = jnp.sum(jnp.where(mine, found[cols : cols + own], 0.0), 0, keepdims=True)
+        for i in range(tile // 128):
             at = start // 128 + i
             piece = slice(i * 128, (i + 1) * 128)
             o_ref[0, at : at + 1, :] = lse[:, piece]
@@ -138,34 +195,32 @@
             o_ref[0, 2 * stat + at : 2 * stat + at + 1, :] = logits[0:1, piece]
 
 
-def joint(enc_all, pred, out_wt, labels, first, used, n_vocab):
+def joint(enc_all, pred, out_wt, label_w, used, n_vocab):
     groups, pad, width = enc_all.shape
     frames = groups * used
-    positions = pred.shape[0]
-    own = positions // n_vocab
+    own = pred.shape[0] // n_vocab
     cols = out_wt.shape[0]
     pairs = own * frames
     stat = 8
-    spread = jnp.broadcast_to(labels.reshape(n_vocab, 1, own, 1), (n_vocab, 1, own, frames))
+    label_w = jnp.pad(label_w.reshape(n_vocab, own, width), ((0, 0), (0, 16 - own), (0, 0)))
     return pl.pallas_call(
         functools.partial(joint_kernel, used),
         grid=(n_vocab,),
         in_specs=[
-            pl.BlockSpec(memory_space=pltpu.SMEM),
             pl.BlockSpec((groups, pad, width), lambda i: (0, 0, 0)),
             pl.BlockSpec((own, width), lambda i: (i, 0)),
             pl.BlockSpec((cols, width), lambda i: (0, 0)),
-            pl.BlockSpec((1, 1, pairs), lambda i: (i, 0, 0)),
+            pl.BlockSpec((1, 16, width), lambda i: (i, 0, 0)),
         ],
         out_specs=pl.BlockSpec((1, 3 * stat, 128), lambda i: (i, 0, 0)),
         out_shape=jax.ShapeDtypeStruct((n_vocab, 3 * stat, 128), F32),
-        scratch_shapes=[pltpu.VMEM((frames, width), F32), pltpu.VMEM((pairs, width), BF)],
+        scratch_shapes=[pltpu.VMEM((frames, width), F32), pltpu.VMEM((cols + 16, width), BF)],
         cost_estimate=pl.CostEstimate(
             flops=2 * n_vocab * pairs * width * cols,
             bytes_accessed=2 * cols * width,
             transcendentals=n_vocab * pairs * (width + cols),
         ),
-    )(first, enc_all, pred, out_wt, spread.reshape(n_vocab, 1, pairs))
+    )(enc_all, pred, out_wt, label_w)
 
 
 def local(
@@ -196,11 +251,10 @@
         jnp.broadcast_to(queries[None], (n_peers,) + queries.shape), PEERS, 0, 0, tiled=True
     )
 
-    phrase_vec = encode_local(phrase_ids, phrase_lens, phrase_table, phrase_w)
-    other_vec = lax.ppermute(phrase_vec, "c", [(0, 1), (1, 0)])
-    vecs = jnp.concatenate([phrase_vec, other_vec], 0)
-    keys = mm(vecs, key_w).astype(BF)
-    values = mm(vecs, value_w).astype(BF)
+    swap = [(0, 1), (1, 0)]
+    ids = jnp.concatenate([phrase_ids, lax.ppermute(phrase_ids, "c", swap)], 0)
+    lens = jnp.concatenate([phrase_lens, lax.ppermute(phrase_lens, "c", swap)], 0)
+    keys, values = encode(ids, lens, phrase_table, phrase_w, key_w, value_w)
 
     utts, positions = labels.shape
     frames_dev = used * n_vocab
@@ -210,18 +264,17 @@
     own_labels = lax.dynamic_slice_in_dim(labels, utt, 1, 0)[0]
     picked = jnp.concatenate([jnp.zeros((1,), jnp.int32), own_labels[:-1]])
     predictor = mm(pred_table[picked], pred_w).astype(BF).astype(F32)
+    vocab_index = lax.axis_index(VOCAB)
+    cols = out_w.shape[1]
     out_wt = out_w.T
+    column = vocab_index * cols + jnp.arange(cols, dtype=jnp.int32)
+    label_w = mm((own_labels[:, None] == column[None, :]).astype(BF), out_wt).astype(BF)
 
     parts = attend(asked.reshape(n_peers * PAD, -1), keys, values, used)
     parts = lax.all_to_all(parts.reshape(n_peers, PAD, -1), PEERS, 0, 0, tiled=True)
-    enc = join(parts, frames_pad, context_w, joint_enc_w, used)
-    enc_all = lax.all_to_all(
-        jnp.broadcast_to(enc[None], (n_vocab,) + enc.shape), VOCAB, 0, 0, tiled=True
-    )
-    vocab_index = lax.axis_index(VOCAB)
-    cols = out_w.shape[1]
-    first = (vocab_index * cols).astype(jnp.int32).reshape(1)
-    stats = joint(enc_all, predictor, out_wt, own_labels, first, used, n_vocab)
+    enc = join(parts, frames_pad, context_w, joint_enc_w, used, n_vocab)
+    enc_all = lax.all_to_all(enc, VOCAB, 0, 0, tiled=True)
+    stats = joint(enc_all, predictor, out_wt, label_w, used, n_vocab)
     stats = lax.all_to_all(stats, VOCAB, 0, 0, tiled=True)
 
     own = positions // n_vocab

time: 141 us -> 118 us (0.84)
  local copies, waits for them, and re-layouts: 36.5 us -> 15.5 us
  Pallas kernels: 27 us -> 40.2 us
  waiting for transfers between devices: 34.4 us -> 24 us
  matrix products: 11.7 us -> 3.4 us
  starting transfers between devices: 25.1 us -> 29.3 us
    gather x1 -> x0, local copies, waits for them, and re-layouts: 20.2 us -> none  [encode_local(): emb = phrase_table[ids]]
    pallas_call x0 -> x1, Pallas kernels: none -> 15.1 us  [encode(): pl.pallas_call(encode_kernel, grid=(phrases // tile,), in_specs=[pl.Block...]
    all_to_all x1, waiting for transfers between devices: 13.6 us -> 0.01 us  [local(): lax.all_to_all(jnp.broadcast_to(queries[None], (n_peers,) + queries.shape...]
    all_to_all x1, starting transfers between devices: 5.19 us -> 10.4 us  [local(): lax.all_to_all(parts.reshape(n_peers, PAD, -1), PEERS, 0, 0, tiled=True)]
    dot_general x5 -> x3, matrix products: 8.27 us -> 3.4 us  [mm(): return jnp.dot(a, b, preferred_element_type=F32)]
    dot_general x1 -> x0, matrix products: 3.48 us -> none  [encode_local(): summed = jnp.einsum('npe,np->ne', emb, mask, preferred_element_type=F32)]
    broadcast_in_dim x5 -> x0, local copies, waits for them, and re-layouts: 2.42 us -> none  [the longest x1 1.41 us: local(): jnp.broadcast_to(enc[None], (n_vocab,) + enc.shape)]
    pallas_call x1, Pallas kernels: 12 us -> 9.87 us  [attend(): pl.pallas_call(functools.partial(attend_kernel, used, 1.0 / math.sqrt(hea...]
  transfers between devices with their start and end apart: 5 -> 6, of which waited for: 4 -> 3; matrix products, arithmetic and copies ran while one was open for 14% -> 13% of each run, Pallas kernels for 0% -> 13%
where the time goes in v2:
time: 118 us; the launch traced here: 117 us
  Pallas kernels  40.2 us (34%)
  starting transfers between devices  29.3 us (25%)
  waiting for transfers between devices  24 us (20%)
  local copies, waits for them, and re-layouts  15.5 us (13%)
  other arithmetic  3.57 us (3%)
  matrix products  3.4 us (3%)
    pallas_call x1, Pallas kernels, encode(): pl.pallas_call(encode_kernel, grid=(phrases // tile,), in_specs=[pl.Block...  15.1 us
    all_to_all x1, waiting for transfers between devices, local(): lax.all_to_all(parts.reshape(n_peers, PAD, -1), PEERS, 0, 0, tiled=True)  12.9 us
    all_to_all x1, starting transfers between devices, local(): lax.all_to_all(jnp.broadcast_to(queries[None], (n_peers,) + queries.shape...  11.5 us
    pallas_call x1, Pallas kernels, joint(): pl.pallas_call(functools.partial(joint_kernel, used), grid=(n_vocab,), in...  11.2 us
    all_to_all x1, starting transfers between devices, local(): lax.all_to_all(parts.reshape(n_peers, PAD, -1), PEERS, 0, 0, tiled=True)  10.4 us
    pallas_call x1, Pallas kernels, attend(): pl.pallas_call(functools.partial(attend_kernel, used, 1.0 / math.sqrt(hea...  9.87 us
    all_to_all x1, waiting for transfers between devices, local(): stats = lax.all_to_all(stats, VOCAB, 0, 0, tiled=True)  7.07 us
    unnamed x17, local copies, waits for them, and re-layouts  4.94 us
  transfers between devices with their start and end apart: 6, of which 3 were waited for; matrix products, arithmetic and copies ran while one was open for 13% of the time, Pallas kernels for 13%

profile of v2, /device:TPU:0, one launch (start us, length us, event | category | flops | bytes accessed | tf_op | source)
XLA Modules:
  0.0 116.8 jit_solution(9928366780647011308)
XLA Ops:
  0.6 1.2 %copy-done = bf16[1024,512]{1,0:T(8,128)(2,1)S(1)} copy-done((bf16[1024,512]{1,0:T(8,128)(2,1)S(1)}, bf16[1024,512]{1,0:T(8,128)(2,1)}, u32[]{:S(2)}) %copy-start) | copy-done | bytes 1048600
  1.9 1.0 convolution_convert_fusion.2
  2.9 1.1 broadcast_in_dim.6
  4.0 11.5 %all-to-all-start = ((bf16[64,16,512]{2,1,0:T(8,128)(2,1)}), bf16[64,16,512]{2,1,0:T(8,128)(2,1)S(1)}, u32[]{:S(2)}, u32[]{:S(2)}) async-start(bf16[64,16,512]{2,1,0:T(8,128)(2,1)} %broadcast_in_dim.6), calls=%async_computation | async-start | bytes 2097152 | tf_op jit(solution)/shard_map/all_to_all | solution.py:250
  15.6 0.5 collective-permute-start.1
  16.1 1.4 %pad.8.frames_ref = bf16[16,1024]{1,0:T(8,128)(2,1)} pad(bf16[12,1024]{1,0:T(8,128)(2,1)} %param.16, bf16[]{:T(256)} %constant.54.clone.1), padding=0_4x0_0 | pad | bytes 57346 | tf_op jit(solution)/shard_map/jit(_pad)/pad | solution.py:248
  17.4 0.7 pad_add_fusion.1
  18.1 1.0 copy.26.lens_ref
  19.2 0.7 pad_add_fusion
  19.9 1.0 copy.25.ids_ref
  20.9 15.1 %shard_map.167 = (bf16[1024,512]{1,0:T(8,128)(2,1)}, bf16[1024,512]{1,0:T(8,128)(2,1)}) custom-call(s32[1024,8]{1,0:T(8,128)} %copy.25.ids_ref, s32[1024,1]{1,0:T(8,128)} %copy.26.lens_ref, bf16[4096,512]{1,0:T(8,128)(2,1)} %table_ref.1, bf16[512,512]{1,0:T(8,128)(2,1)} %phrase_w_ref.1, bf16[512,512]{1,0:T(8,128)(2,1)} %key_w_ref.1, bf16[512,512]{1,0:T(8,128)(2,1)} %value_w_ref.1), custom_call_target="tpu_custom_call" | custom-call | flops 85899345920 | bytes 4194304 | tf_op jit(solution)/shard_map/pallas_call | solution.py:60
  36.0 1.0 copy-done.3
  37.0 9.9 %shard_map.168 = bf16[1024,512]{1,0:T(8,128)(2,1)} custom-call(bf16[1024,512]{1,0:T(8,128)(2,1)} %bitcast.28, bf16[1024,512]{1,0:T(8,128)(2,1)} %get-tuple-element.4.k_ref, bf16[1024,512]{1,0:T(8,128)(2,1)} %get-tuple-element.5.v_ref), custom_call_target="tpu_custom_call" | custom-call | flops 2147483648 | bytes 4194304 | tf_op jit(solution)/shard_map/pallas_call | solution.py:112
  46.8 10.4 %all-to-all-start.1 = ((bf16[64,16,512]{2,1,0:T(8,128)(2,1)}), bf16[64,16,512]{2,1,0:T(8,128)(2,1)S(1)}, u32[]{:S(2)}, u32[]{:S(2)}) async-start(bf16[64,16,512]{2,1,0:T(8,128)(2,1)} %bitcast.29), calls=%async_computation.1 | async-start | bytes 2097152 | tf_op jit(solution)/shard_map/all_to_all | solution.py:274
  57.4 3.9 %gather_fusion = bf16[64,640]{1,0:T(8,128)(2,1)S(1)} fusion(bf16[4096,640]{1,0:T(8,128)(2,1)} %param.29, s32[1024]{0:T(1024)S(1)} %pad_clamp_fusion), kind=kCustom, calls=%fused_computation | custom fusion | bytes 164096 | tf_op jit(solution)/shard_map/gather | solution.py:266
  61.4 2.1 %fusion.pred_ref = f32[64,640]{1,0:T(8,128)} fusion(bf16[64,640]{1,0:T(8,128)(2,1)S(1)} %gather_fusion, bf16[640,640]{1,0:T(8,128)(2,1)} %param.30), kind=kOutput, calls=%fused_computation.3 | convolution fusion | flops 52510720 | bytes 1064960 | tf_op jit(solution)/shard_map/dot_general | solution.py:24
  63.4 12.9 %all-to-all-done.1.parts_ref = bf16[64,16,512]{2,1,0:T(8,128)(2,1)S(1)} async-done(((bf16[64,16,512]{2,1,0:T(8,128)(2,1)}), bf16[64,16,512]{2,1,0:T(8,128)(2,1)S(1)}, u32[]{:S(2)}, u32[]{:S(2)}) %all-to-all-start.1) | async-done | bytes 1048608 | tf_op jit(solution)/shard_map/all_to_all | solution.py:274
  76.4 1.0 copy-done.1
  77.3 4.1 %shard_map.169 = bf16[8,16,640]{2,1,0:T(8,128)(2,1)} custom-call(bf16[64,16,512]{2,1,0:T(8,128)(2,1)} %copy-done.1, bf16[16,1024]{1,0:T(8,128)(2,1)} %pad.8.frames_ref, bf16[512,1024]{1,0:T(8,128)(2,1)} %context_w_ref.1, bf16[1024,640]{1,0:T(8,128)(2,1)} %joint_w_ref.1), custom_call_target="tpu_custom_call" | custom-call | tf_op jit(solution)/shard_map/pallas_call | solution.py:151
  81.4 3.4 %all-to-all-start.2 = ((bf16[8,16,640]{2,1,0:T(8,128)(2,1)}), bf16[8,16,640]{2,1,0:T(8,128)(2,1)S(1)}, u32[]{:S(2)}, u32[]{:S(2)}) async-start(bf16[8,16,640]{2,1,0:T(8,128)(2,1)} %shard_map.169), calls=%async_computation.2 | async-start | bytes 327680 | tf_op jit(solution)/shard_map/all_to_all | solution.py:276
  85.1 1.1 copy.27
  86.2 0.7 pad.9.label_w_ref
  86.9 0.6 dynamic_slice.9
  87.5 0.6 dynamic_slice.10
  88.1 0.7 fusion.8
  88.7 4.0 %all-to-all-done.2.enc_ref = bf16[8,16,640]{2,1,0:T(8,128)(2,1)S(1)} async-done(((bf16[8,16,640]{2,1,0:T(8,128)(2,1)}), bf16[8,16,640]{2,1,0:T(8,128)(2,1)S(1)}, u32[]{:S(2)}, u32[]{:S(2)}) %all-to-all-start.2) | async-done | bytes 163872 | tf_op jit(solution)/shard_map/all_to_all | solution.py:276
  92.8 0.7 copy-done.4
  93.5 11.2 %shard_map.170 = f32[8,24,128]{2,1,0:T(8,128)} custom-call(bf16[8,16,640]{2,1,0:T(8,128)(2,1)} %copy-done.4, f32[64,640]{1,0:T(8,128)} %fusion.pred_ref, bf16[512,640]{1,0:T(8,128)(2,1)} %bitcast.30, bf16[8,16,640]{2,1,0:T(8,128)(2,1)} %pad.9.label_w_ref), custom_call_target="tpu_custom_call" | custom-call | flops 4026531840 | bytes 655360 | tf_op jit(solution)/shard_map/pallas_call | solution.py:206
  104.7 3.4 %all-to-all-start.3 = ((f32[8,24,128]{2,1,0:T(8,128)}), f32[8,24,128]{2,1,0:T(8,128)S(1)}, u32[]{:S(2)}, u32[]{:S(2)}) async-start(f32[8,24,128]{2,1,0:T(8,128)} %shard_map.170), calls=%async_computation.3 | async-start | bytes 196608 | tf_op jit(solution)/shard_map/all_to_all | solution.py:278
  108.0 0.7 add_compare_fusion
  108.7 7.1 %all-to-all-done.3 = f32[8,24,128]{2,1,0:T(8,128)S(1)} async-done(((f32[8,24,128]{2,1,0:T(8,128)}), f32[8,24,128]{2,1,0:T(8,128)S(1)}, u32[]{:S(2)}, u32[]{:S(2)}) %all-to-all-start.3) | async-done | bytes 98336 | tf_op jit(solution)/shard_map/all_to_all | solution.py:278
  116.2 0.7 select_bitcast_fusion
  (31 shorter events, 0.9 us)
Async XLA Ops:
  0.6 1.2 %copy-start = (bf16[1024,512]{1,0:T(8,128)(2,1)S(1)}, bf16[1024,512]{1,0:T(8,128)(2,1)}, u32[]{:S(2)}) copy-start(bf16[1024,512]{1,0:T(8,128)(2,1)} %param.26) | copy-start | bytes 3145732
  4.0 32.0 %all-to-all-start = ((bf16[64,16,512]{2,1,0:T(8,128)(2,1)}), bf16[64,16,512]{2,1,0:T(8,128)(2,1)S(1)}, u32[]{:S(2)}, u32[]{:S(2)}) async-start(bf16[64,16,512]{2,1,0:T(8,128)(2,1)} %broadcast_in_dim.6), calls=%async_computation | async-start | bytes 2097152 | tf_op jit(solution)/shard_map/all_to_all | solution.py:250
  15.5 3.7 %collective-permute-start = (s32[512,8]{0,1:T(8,128)}, s32[512,8]{0,1:T(8,128)S(1)}, u32[]{:S(2)}, u32[]{:S(2)}) collective-permute-start(s32[512,8]{0,1:T(8,128)} %param.20), channel_id=1, source_target_pairs={{0,8},{8,0},{1,9},{9,1},{2,10},{10,2},{3,11},{11,3},{4,12},{12,4},... | collective-permute-start | bytes 49160 | tf_op jit(solution)/shard_map/ppermute | solution.py:255
  15.6 1.9 %collective-permute-start.1 = (s32[512]{0:T(512)}, s32[512]{0:T(512)S(1)}, u32[]{:S(2)}, u32[]{:S(2)}) collective-permute-start(s32[512]{0:T(512)} %param.21), channel_id=1, source_target_pairs={{0,8},{8,0},{1,9},{9,1},{2,10},{10,2},{3,11},{11,3},{4,12},{12,4},... | collective-permute-start | bytes 6152 | tf_op jit(solution)/shard_map/ppermute | solution.py:256
  36.0 21.3 %copy-start.5 = (s32[4,64]{1,0:T(4,128)S(1)}, s32[4,64]{1,0:T(4,128)}, u32[]{:S(2)}) copy-start(s32[4,64]{1,0:T(4,128)} %param.18) | copy-start | bytes 3076
  36.0 1.0 copy-start.3
  46.8 38.0 %copy-start.2 = (bf16[640,512]{1,0:T(8,128)(2,1)S(1)}, bf16[640,512]{1,0:T(8,128)(2,1)}, u32[]{:S(2)}) copy-start(bf16[640,512]{1,0:T(8,128)(2,1)} %param.31) | copy-start | bytes 1966084
  46.8 40.1 %copy-start.6 = (s32[4]{0:T(128)S(1)}, s32[4]{0:T(128)}, u32[]{:S(2)}) copy-start(s32[4]{0:T(128)} %param.17) | copy-start | bytes 52
  46.8 40.7 %copy-start.7 = (s32[4]{0:T(128)S(1)}, s32[4]{0:T(128)}, u32[]{:S(2)}) copy-start(s32[4]{0:T(128)} %param.19) | copy-start | bytes 52
  46.8 29.5 %all-to-all-start.1 = ((bf16[64,16,512]{2,1,0:T(8,128)(2,1)}), bf16[64,16,512]{2,1,0:T(8,128)(2,1)S(1)}, u32[]{:S(2)}, u32[]{:S(2)}) async-start(bf16[64,16,512]{2,1,0:T(8,128)(2,1)} %bitcast.29), calls=%async_computation.1 | async-start | bytes 2097152 | tf_op jit(solution)/shard_map/all_to_all | solution.py:274
  76.4 1.0 copy-start.1
  81.4 11.4 %all-to-all-start.2 = ((bf16[8,16,640]{2,1,0:T(8,128)(2,1)}), bf16[8,16,640]{2,1,0:T(8,128)(2,1)S(1)}, u32[]{:S(2)}, u32[]{:S(2)}) async-start(bf16[8,16,640]{2,1,0:T(8,128)(2,1)} %shard_map.169), calls=%async_computation.2 | async-start | bytes 327680 | tf_op jit(solution)/shard_map/all_to_all | solution.py:276
  92.8 0.7 copy-start.4
  104.7 11.1 %all-to-all-start.3 = ((f32[8,24,128]{2,1,0:T(8,128)}), f32[8,24,128]{2,1,0:T(8,128)S(1)}, u32[]{:S(2)}, u32[]{:S(2)}) async-start(f32[8,24,128]{2,1,0:T(8,128)} %shard_map.170), calls=%async_computation.3 | async-start | bytes 196608 | tf_op jit(solution)/shard_map/all_to_all | solution.py:278

commit v3 on v2

v3 whole, which is shorter than its diff:
```python
import functools
import math

import jax
import jax.numpy as jnp
from jax import lax
from jax.experimental import pallas as pl
from jax.experimental.pallas import tpu as pltpu
from jax.sharding import Mesh, PartitionSpec as P

HEADS = 4
PAD = 16
AXES = ("y", "zl", "c", "x", "zh")
PHRASE = ("y", "zl", "c")
VOCAB = ("x", "zh")
PEERS = ("y", "zl", "x", "zh")
BF = jnp.bfloat16
F32 = jnp.float32
LOG2E = 1.0 / math.log(2.0)
NT = (((1,), (1,)), ((), ()))


def mm(a, b):
    return jnp.dot(a, b, preferred_element_type=F32)


def encode_kernel(ids_ref, table_ref, phrase_w_ref, key_w_ref, value_w_ref, o_ref):
    rows, tokens = ids_ref.shape
    vocab = table_ref.shape[0]
    ids = ids_ref[...]
    lens = jnp.sum(jnp.where(ids >= 0, 1.0, 0.0), 1, keepdims=True)
    lane = lax.broadcasted_iota(jnp.int32, (rows, 128), 1)
    blocks, units = [], []
    for t in range(tokens):
        token = jnp.broadcast_to(ids[:, t : t + 1], (rows, 128))
        blocks.append(lax.shift_right_arithmetic(token, 7).astype(F32).astype(BF))
        units.append(jnp.where((token & 127) == lane, 1.0, 0.0).astype(BF))
    zero = jnp.zeros((rows, 128), BF)
    summed = jnp.zeros((rows, table_ref.shape[1]), F32)
    for pair in range(vocab // 256):
        counts = []
        for block in (2 * pair, 2 * pair + 1):
            count = zero
            for t in range(tokens):
                count += jnp.where(blocks[t] == BF(block), units[t], zero)
            counts.append(count)
        summed += mm(jnp.concatenate(counts, 1), table_ref[pair * 256 : (pair + 1) * 256, :])
    mean = (summed / lens).astype(BF)
    vec = jnp.tanh(mm(mean, phrase_w_ref[...])).astype(BF)
    width = key_w_ref.shape[1]
    o_ref[:, :width] = mm(vec, key_w_ref[...]).astype(BF)
    o_ref[:, width:] = mm(vec, value_w_ref[...]).astype(BF)


def encode(ids, table, phrase_w, key_w, value_w):
    phrases, tokens = ids.shape
    vocab, width = table.shape
    tile = 256
    whole = lambda a: pl.BlockSpec(a.shape, lambda i: (0, 0))
    return pl.pallas_call(
        encode_kernel,
        grid=(phrases // tile,),
        in_specs=[
            pl.BlockSpec((tile, tokens), lambda i: (i, 0)),
            whole(table),
            whole(phrase_w),
            whole(key_w),
            whole(value_w),
        ],
        out_specs=pl.BlockSpec((tile, 2 * width), lambda i: (i, 0)),
        out_shape=jax.ShapeDtypeStruct((phrases, 2 * width), BF),
        cost_estimate=pl.CostEstimate(
            flops=40 * phrases * vocab * width,
            bytes_accessed=2 * vocab * width,
            transcendentals=phrases * width,
        ),
    )(ids, table, phrase_w, key_w, value_w)


def attend_kernel(used, scale, q_ref, k0_ref, v0_ref, k1_ref, v1_ref, o_ref):
    rows, tile = q_ref.shape[0], 256
    k = jnp.concatenate([k0_ref[...], k1_ref[...]], 0)
    v = jnp.concatenate([v0_ref[...], v1_ref[...]], 0)
    head = v.shape[1]
    v_ones = jnp.concatenate([v, jnp.ones_like(v)], 1)
    for start in range(0, rows, tile):
        q = q_ref[start : start + tile, :]
        scores = lax.dot_general(q, k, NT, preferred_element_type=F32)
        peak = jnp.max(scores, -1, keepdims=True)
        weights = jnp.exp2((scores - peak) * (scale * LOG2E)).astype(BF)
        sums = mm(weights, v_ones)
        total = sums[:, head:]
        part = sums[:, :head] / total
        rest = peak * scale + jnp.log(total)
        groups = tile // PAD
        shape = (groups, PAD, part.shape[1])
        row = lax.broadcasted_iota(jnp.int32, shape, 1)
        lane = lax.broadcasted_iota(jnp.int32, shape, 2)
        part = part.reshape(shape)
        for piece in range(3):
            sent = rest.astype(BF).astype(F32)
            rest = rest - sent
            line = jnp.sum(jnp.where(lane == row, sent.reshape(shape), 0.0), 1, keepdims=True)
            part = jnp.where(row == used + piece, line, part)
        o_ref[start : start + tile, :] = part.reshape(tile, shape[2]).astype(BF)


def attend(asked, both, other, used):
    rows, width = asked.shape
    head = width // HEADS
    phrases = both.shape[0]
    keys = pl.BlockSpec((phrases, head), lambda h: (0, h))
    values = pl.BlockSpec((phrases, head), lambda h: (0, HEADS + h))
    return pl.pallas_call(
        functools.partial(attend_kernel, used, 1.0 / math.sqrt(head)),
        grid=(HEADS,),
        in_specs=[
            pl.BlockSpec((rows, head), lambda h: (0, h)),
            keys,
            values,
            keys,
            values,
        ],
        out_specs=pl.BlockSpec((rows, head), lambda h: (0, h)),
        out_shape=jax.ShapeDtypeStruct((rows, width), BF),
        cost_estimate=pl.CostEstimate(
            flops=8 * rows * phrases * width,
            bytes_accessed=4 * rows * width + 8 * phrases * width,
            transcendentals=2 * rows * phrases * HEADS,
        ),
    )(asked, both, both, other, other)


def joint_kernel(
    used, parts_ref, frames_ref, context_w_ref, joint_w_ref, pred_ref, label_w_ref, w_ref, o_ref,
    rows_s, lse_s, found_s,
):
    step = pl.program_id(0)
    count = rows_s.shape[0]
    positions = pred_ref.shape[0]
    groups = o_ref.shape[0]
    own = positions // groups
    pairs = own * used

    @pl.when(step == 0)
    def _():
        peers, pad, width = parts_ref.shape
        head = width // HEADS
        row = lax.broadcasted_iota(jnp.int32, (peers, pad, head), 1)
        lane = lax.broadcasted_iota(jnp.int32, (peers, pad, head), 2)
        columns = []
        for h in range(HEADS):
            block = parts_ref[:, :, h * head : (h + 1) * head].astype(F32)
            lse = jnp.sum(jnp.where((row >= used) & (row < used + 3), block, 0.0), 1, keepdims=True)
            factor = jnp.exp(lse - jnp.max(lse, 0, keepdims=True))
            factor = factor / jnp.sum(factor, 0, keepdims=True)
            weight = jnp.sum(jnp.where(lane == row, factor, 0.0), -1, keepdims=True)
            columns.append(jnp.sum(weight * block, 0))
        context = jnp.concatenate(columns, 1).astype(BF)
        biased = (frames_ref[...].astype(F32) + mm(context, context_w_ref[...])).astype(BF)
        enc = mm(biased, joint_w_ref[...]).astype(BF).astype(F32)
        for g in range(groups):
            pred = pred_ref[g * own : (g + 1) * own, :]
            for f in range(0, used, 2):
                pair = jnp.concatenate([pred + enc[f : f + 1, :], pred + enc[f + 1 : f + 2, :]], 0)
                at = g * pairs + f * own
                rows_s[at : at + 2 * own, :] = jnp.tanh(pair).astype(BF)
        found = lax.dot_general(label_w_ref[...], rows_s[...], NT, preferred_element_type=F32)
        at = lax.broadcasted_iota(jnp.int32, found.shape, 1)
        position = (at // pairs) * own + at % own
        mine = position == lax.broadcasted_iota(jnp.int32, found.shape, 0)
        found_s[0:1, :] = jnp.sum(jnp.where(mine, found, 0.0), 0, keepdims=True)

    tile = 256
    for start in range(0, count, tile):
        rows = rows_s[start : start + tile, :]
        logits = lax.dot_general(w_ref[...], rows, NT, preferred_element_type=F32)
        peak = jnp.max(logits, 0, keepdims=True)
        total = jnp.sum(jnp.exp2((logits - peak) * LOG2E), 0, keepdims=True)
        lse_s[pl.ds(step, 1), start : start + tile] = peak + jnp.log(total)

        @pl.when(step == 0)
        def _():
            found_s[1:2, start : start + tile] = logits[0:1]

    @pl.when(step == pl.num_programs(0) - 1)
    def _():
        lse = lse_s[...]
        peak = jnp.max(lse, 0, keepdims=True)
        norm = peak + jnp.log(jnp.sum(jnp.exp(lse - peak), 0, keepdims=True))
        label = found_s[0:1, :] - norm
        blank = found_s[1:2, :] - norm
        for g in range(groups):
            piece = slice(g * pairs, (g + 1) * pairs)
            o_ref[g, 0:1, :pairs] = blank[:, piece]
            o_ref[g, 1:2, :pairs] = label[:, piece]


def joint(parts, frames, context_w, joint_w, pred, label_w, out_wt, used, groups):
    vocab, width = out_wt.shape
    positions = pred.shape[0]
    count = positions * used
    block = 512
    whole = lambda a: pl.BlockSpec(a.shape, lambda i: (0,) * a.ndim)
    return pl.pallas_call(
        functools.partial(joint_kernel, used),
        grid=(vocab // block,),
        in_specs=[whole(a) for a in (parts, frames, context_w, joint_w, pred, label_w)]
        + [pl.BlockSpec((block, width), lambda i: (i, 0))],
        out_specs=pl.BlockSpec((groups, 2, 128), lambda i: (0, 0, 0)),
        out_shape=jax.ShapeDtypeStruct((groups, 2, 128), F32),
        scratch_shapes=[
            pltpu.VMEM((count, width), BF),
            pltpu.VMEM((vocab // block, count), F32),
            pltpu.VMEM((8, count), F32),
        ],
        cost_estimate=pl.CostEstimate(
            flops=2 * count * width * vocab,
            bytes_accessed=2 * vocab * width,
            transcendentals=count * vocab,
        ),
    )(parts, frames, context_w, joint_w, pred, label_w, out_wt)


def local(
    frames,
    frame_lens,
    labels,
    label_lens,
    phrase_ids,
    phrase_lens,
    phrase_table,
    phrase_w,
    key_w,
    value_w,
    query_w,
    context_w,
    joint_enc_w,
    pred_table,
    pred_w,
    out_w,
):
    n_vocab = lax.axis_size(VOCAB)
    n_phrase = lax.axis_size(PHRASE)
    n_peers = lax.axis_size(PEERS)
    used = frames.shape[0]
    out_wt = lax.all_gather(out_w.T, VOCAB, axis=0, tiled=True)
    frames_pad = jnp.pad(frames, ((0, PAD - used), (0, 0)))
    queries = mm(frames_pad, query_w).astype(BF)
    asked = lax.all_to_all(
        jnp.broadcast_to(queries[None], (n_peers,) + queries.shape), PEERS, 0, 0, tiled=True
    )

    swap = [(0, 1), (1, 0)]
    slot = jnp.arange(phrase_ids.shape[1], dtype=jnp.int32)
    ids = jnp.where(slot[None, :] < phrase_lens[:, None], phrase_ids, -1)
    both = encode(ids, phrase_table, phrase_w, key_w, value_w)
    other = lax.ppermute(both, "c", swap)

    utts, positions = labels.shape
    frames_dev = used * n_vocab
    tlen = frames_dev * n_phrase // utts
    start = lax.axis_index(PHRASE) * frames_dev
    utt = start // tlen
    own_labels = lax.dynamic_slice_in_dim(labels, utt, 1, 0)[0]
    picked = jnp.concatenate([jnp.zeros((1,), jnp.int32), own_labels[:-1]])
    predictor = mm(pred_table[picked], pred_w).astype(BF).astype(F32)
    label_w = out_wt[own_labels]

    parts = attend(asked.reshape(n_peers * PAD, -1), both, other, used)
    parts = lax.all_to_all(parts.reshape(n_peers, PAD, -1), PEERS, 0, 0, tiled=True)
    logp = joint(
        parts, frames_pad, context_w, joint_enc_w, predictor, label_w, out_wt, used, n_vocab
    )
    logp = lax.all_to_all(logp, VOCAB, 0, 0, tiled=True)

    own = positions // n_vocab
    logp = logp[:, :, : own * used].reshape(n_vocab, 2, used, own)
    blank = logp[:, 0].reshape(frames_dev, own)
    label = logp[:, 1].reshape(frames_dev, own)
    moment = start % tlen + jnp.arange(frames_dev, dtype=jnp.int32)
    position = lax.axis_index(VOCAB) * own + jnp.arange(own, dtype=jnp.int32)
    frame_len = lax.dynamic_slice_in_dim(frame_lens, utt, 1, 0)
    label_len = lax.dynamic_slice_in_dim(label_lens, utt, 1, 0)
    live = (moment < frame_len)[:, None]
    blank_out = jnp.where(live & (position <= label_len)[None, :], blank, 0.0)
    label_out = jnp.where(live & (position < label_len)[None, :], label, 0.0)
    return (blank_out, label_out)


def solution(mesh):
    n_phrase, n_vocab = mesh.devices.shape
    fine = Mesh(mesh.devices.reshape(n_phrase // 4, 2, 2, n_vocab // 2, 2), AXES)
    rows = P(AXES, None)
    in_specs = (
        rows,
        P(),
        P(),
        P(),
        rows,
        P(AXES),
        P(),
        P(),
        P(),
        P(),
        P(),
        P(),
        P(),
        P(),
        P(),
        P(None, VOCAB),
    )
    out_specs = (P(PHRASE, VOCAB), P(PHRASE, VOCAB))
    return jax.shard_map(local, mesh=fine, in_specs=in_specs, out_specs=out_specs, check_vma=False)
```

time: 118 us -> 158 us (1.34)
  waiting for transfers between devices: 24 us -> 60.2 us
  between operations: 0.81 us -> 14.2 us
  starting transfers between devices: 29.3 us -> 20.3 us
  matrix products: 3.4 us -> 1.16 us
  local copies, waits for them, and re-layouts: 15.5 us -> 17.4 us
    all_gather x0 -> x1, waiting for transfers between devices: none -> 32.6 us  [local(): out_wt = lax.all_gather(out_w.T, VOCAB, axis=0, tiled=True)]
    all_to_all x1, waiting for transfers between devices: 0.01 us -> 20.7 us  [local(): lax.all_to_all(jnp.broadcast_to(queries[None], (n_peers,) + queries.shape...]
    all_to_all x1, waiting for transfers between devices: 12.9 us -> 0.01 us  [local(): lax.all_to_all(parts.reshape(n_peers, PAD, -1), PEERS, 0, 0, tiled=True)]
    pallas_call x1, Pallas kernels: 15.1 us -> 9.02 us  [encode(): pl.pallas_call(encode_kernel, grid=(phrases // tile,), in_specs=[pl.Block...]
    pallas_call x2 -> x1, Pallas kernels: 15.3 us -> 20.7 us  [joint(): pl.pallas_call(functools.partial(joint_kernel, used), grid=(vocab // bloc...]
    all_to_all x1, starting transfers between devices: 10.4 us -> 5.47 us  [local(): lax.all_to_all(parts.reshape(n_peers, PAD, -1), PEERS, 0, 0, tiled=True)]
    gather x0 -> x1, local copies, waits for them, and re-layouts: none -> 4.51 us  [local(): label_w = out_wt[own_labels]]
    all_to_all x2 -> x1, waiting for transfers between devices: 11.1 us -> 6.95 us  [local(): logp = lax.all_to_all(logp, VOCAB, 0, 0, tiled=True)]
  transfers between devices with their start and end apart: 6 -> 5, of which waited for: 3 -> 3; matrix products, arithmetic and copies ran while one was open for 13% -> 11% of each run, Pallas kernels for 13% -> 12%
where the time goes in v3:
time: 158 us; the launch traced here: 157 us
  waiting for transfers between devices  60.2 us (38%)
  Pallas kernels  39.8 us (25%)
  starting transfers between devices  20.3 us (13%)
  local copies, waits for them, and re-layouts  17.4 us (11%)
  between operations  14.2 us (9%)
  other arithmetic  4.3 us (3%)
    all_gather x1, waiting for transfers between devices, local(): out_wt = lax.all_gather(out_w.T, VOCAB, axis=0, tiled=True)  32.6 us
    pallas_call x1, Pallas kernels, joint(): pl.pallas_call(functools.partial(joint_kernel, used), grid=(vocab // bloc...  20.7 us
    all_to_all x1, waiting for transfers between devices, local(): lax.all_to_all(jnp.broadcast_to(queries[None], (n_peers,) + queries.shape...  20.7 us
    all_to_all x1, starting transfers between devices, local(): lax.all_to_all(jnp.broadcast_to(queries[None], (n_peers,) + queries.shape...  11.5 us
    pallas_call x1, Pallas kernels, attend(): pl.pallas_call(functools.partial(attend_kernel, used, 1.0 / math.sqrt(hea...  10.1 us
    pallas_call x1, Pallas kernels, encode(): pl.pallas_call(encode_kernel, grid=(phrases // tile,), in_specs=[pl.Block...  9.02 us
    all_to_all x1, waiting for transfers between devices, local(): logp = lax.all_to_all(logp, VOCAB, 0, 0, tiled=True)  6.95 us
    unnamed x18, local copies, waits for them, and re-layouts  5.48 us
  transfers between devices with their start and end apart: 5, of which 3 were waited for; matrix products, arithmetic and copies ran while one was open for 11% of the time, Pallas kernels for 12%

profile of v3, /device:TPU:0, one launch (start us, length us, event | category | flops | bytes accessed | tf_op | source)
XLA Modules:
  0.0 157.4 jit_solution(3971735732785248328)
XLA Ops:
  7.2 2.2 %copy.28 = bf16[640,512]{0,1:T(8,128)(2,1)} copy(bf16[640,512]{1,0:T(8,128)(2,1)} %param.31) | data formatting | bytes 1310720 | tf_op args[15]
  9.5 0.8 copy.27
  10.3 1.5 fusion.1.ids_ref
  11.9 9.0 %shard_map.167.k0_ref.v0_ref = bf16[512,1024]{1,0:T(8,128)(2,1)} custom-call(s32[512,8]{1,0:T(8,128)} %fusion.1.ids_ref, bf16[4096,512]{1,0:T(8,128)(2,1)} %table_ref.1, bf16[512,512]{1,0:T(8,128)(2,1)} %phrase_w_ref.1, bf16[512,512]{1,0:T(8,128)(2,1)} %key_w_ref.1, bf16[512,512]{1,0:T(8,128)(2,1)} %value_w_ref.1), custom_call_target="tpu_custom_call" | custom-call | flops 42949672960 | bytes 4194304 | tf_op jit(solution)/shard_map/pallas_call | solution.py:60
  20.9 0.2 convolution_convert_fusion.1
  21.2 1.1 broadcast_in_dim.10
  22.3 11.5 %all-to-all-start = ((bf16[64,16,512]{2,1,0:T(8,128)(2,1)}), bf16[64,16,512]{2,1,0:T(8,128)(2,1)S(1)}, u32[]{:S(2)}, u32[]{:S(2)}) async-start(bf16[64,16,512]{2,1,0:T(8,128)(2,1)} %broadcast_in_dim.10), calls=%async_computation | async-start | bytes 2097152 | tf_op jit(solution)/shard_map/all_to_all | solution.py:250
  33.8 0.6 pad.4.frames_ref
  34.4 0.6 dynamic_slice.9
  35.0 0.6 dynamic_slice.10
  35.6 20.7 %all-to-all-done = bf16[64,16,512]{2,1,0:T(8,128)(2,1)S(1)} async-done(((bf16[64,16,512]{2,1,0:T(8,128)(2,1)}), bf16[64,16,512]{2,1,0:T(8,128)(2,1)S(1)}, u32[]{:S(2)}, u32[]{:S(2)}) %all-to-all-start) | async-done | bytes 1048608 | tf_op jit(solution)/shard_map/all_to_all | solution.py:250
  56.3 1.1 copy-done.5
  57.4 0.3 copy-done.1
  57.7 10.1 %shard_map.168 = bf16[1024,512]{1,0:T(8,128)(2,1)} custom-call(bf16[1024,512]{1,0:T(8,128)(2,1)} %bitcast.28, bf16[512,1024]{1,0:T(8,128)(2,1)} %shard_map.167.k0_ref.v0_ref, bf16[512,1024]{1,0:T(8,128)(2,1)} %shard_map.167.k0_ref.v0_ref, bf16[512,1024]{1,0:T(8,128)(2,1)} %copy-done.5, bf16[512,1024]{1,0:T(8,128)(2,1)} %copy-done.5), custom_call_target="tpu_custom_call" | custom-call | flops 2147483648 | bytes 4194304 | tf_op jit(solution)/shard_map/pallas_call | solution.py:114
  67.8 5.5 %all-to-all-start.1 = ((bf16[64,16,512]{2,1,0:T(8,128)(2,1)}), bf16[64,16,512]{2,1,0:T(8,128)(2,1)S(1)}, u32[]{:S(2)}, u32[]{:S(2)}) async-start(bf16[64,16,512]{2,1,0:T(8,128)(2,1)} %bitcast.29), calls=%async_computation.1 | async-start | bytes 2097152 | tf_op jit(solution)/shard_map/all_to_all | solution.py:271
  73.2 0.7 fusion.3
  73.9 0.1 fusion.2
  74.0 4.0 %gather_fusion = bf16[64,640]{1,0:T(8,128)(2,1)S(1)} fusion(bf16[4096,640]{1,0:T(8,128)(2,1)} %param.29, s32[1024]{0:T(1024)S(1)} %pad_clamp_fusion.1), kind=kCustom, calls=%fused_computation | custom fusion | bytes 164096 | tf_op jit(solution)/shard_map/gather | solution.py:267
  78.0 0.7 fusion.4
  78.7 0.9 fusion.pred_ref
  79.6 32.6 %all-gather.2.cloned.1.call-done.w_ref = bf16[4096,640]{1,0:T(8,128)(2,1)} async-done(((bf16[512,640]{1,0:T(8,128)(2,1)}), bf16[4096,640]{1,0:T(8,128)(2,1)}) %all-gather.2.cloned.1.call-update) | async-done | bytes 5242896 | tf_op jit(solution)/shard_map/all_gather | solution.py:247
  112.2 4.5 %gather_fusion.1 = bf16[64,640]{1,0:T(8,128)(2,1)} fusion(bf16[4096,640]{1,0:T(8,128)(2,1)} %all-gather.2.cloned.1.call-done.w_ref, s32[1024]{0:T(1024)S(1)} %pad_clamp_fusion), kind=kCustom, calls=%fused_computation.1 | custom fusion | bytes 164096 | tf_op jit(solution)/shard_map/gather | solution.py:268
  116.7 1.0 copy-done.2
  117.7 20.7 %shard_map.169 = f32[8,2,128]{2,1,0:T(2,128)} custom-call(bf16[64,16,512]{2,1,0:T(8,128)(2,1)} %copy-done.2, bf16[16,1024]{1,0:T(8,128)(2,1)} %pad.4.frames_ref, bf16[512,1024]{1,0:T(8,128)(2,1)} %context_w_ref.1, bf16[1024,640]{1,0:T(8,128)(2,1)} %joint_w_ref.1, f32[64,640]{1,0:T(8,128)} %fusion.pred_ref, bf16[64,640]{1,0:T(8,128)(2,1)} %gather_fusion.1, ...), custom_call_target="tpu_custom_call" | custom-call | flops 4026531840 | bytes 5242880 | tf_op jit(solution)/shard_map/pallas_call | solution.py:205
  138.4 3.3 %all-to-all-start.2 = ((f32[8,2,128]{2,1,0:T(2,128)}), f32[8,2,128]{2,1,0:T(2,128)S(1)}, u32[]{:S(2)}, u32[]{:S(2)}) async-start(f32[8,2,128]{2,1,0:T(2,128)} %shard_map.169), calls=%async_computation.2 | async-start | bytes 16384 | tf_op jit(solution)/shard_map/all_to_all | solution.py:275
  141.7 0.7 add_compare_fusion
  142.4 6.9 %all-to-all-done.2 = f32[8,2,128]{2,1,0:T(2,128)S(1)} async-done(((f32[8,2,128]{2,1,0:T(2,128)}), f32[8,2,128]{2,1,0:T(2,128)S(1)}, u32[]{:S(2)}, u32[]{:S(2)}) %all-to-all-start.2) | async-done | bytes 8224 | tf_op jit(solution)/shard_map/all_to_all | solution.py:275
  149.3 0.1 reshape.134
  149.5 0.1 copy.31
  149.6 0.1 reshape_squeeze.7
  149.7 0.1 copy.30
  149.9 0.7 and_select_fusion
  (24 shorter events, 0.2 us)
Async XLA Ops:
  7.2 13.7 %copy-start = (bf16[1024,512]{1,0:T(8,128)(2,1)S(1)}, bf16[1024,512]{1,0:T(8,128)(2,1)}, u32[]{:S(2)}) copy-start(bf16[1024,512]{1,0:T(8,128)(2,1)} %param.26) | copy-start | bytes 3145732
  7.2 105.0 %all-gather.2.cloned.1.call-start = ((), (), s32[]{:S(2)}) async-start(), calls=%async_computation.3 | async-start | bytes 5898240 | tf_op jit(solution)/shard_map/all_gather | solution.py:247
  11.9 9.0 %copy-start.4 = (bf16[12,1024]{1,0:T(8,128)(2,1)S(1)}, bf16[12,1024]{1,0:T(8,128)(2,1)}, u32[]{:S(2)}) copy-start(bf16[12,1024]{1,0:T(8,128)(2,1)} %param.16) | copy-start | bytes 73732
  11.9 22.6 %copy-start.6 = (s32[4]{0:T(128)S(1)}, s32[4]{0:T(128)}, u32[]{:S(2)}) copy-start(s32[4]{0:T(128)} %param.17) | copy-start | bytes 52
  11.9 23.2 %copy-start.7 = (s32[4]{0:T(128)S(1)}, s32[4]{0:T(128)}, u32[]{:S(2)}) copy-start(s32[4]{0:T(128)} %param.19) | copy-start | bytes 52
  20.9 35.4 %collective-permute-start = (bf16[512,1024]{1,0:T(8,128)(2,1)}, bf16[512,1024]{1,0:T(8,128)(2,1)S(1)}, u32[]{:S(2)}, u32[]{:S(2)}) collective-permute-start(bf16[512,1024]{1,0:T(8,128)(2,1)} %shard_map.167.k0_ref.v0_ref), channel_id=1, source_target_pairs={{0,8},{8,0},{1,9},{9,1},{2,10},{10,2},{3,11},{11,3},{4,12},{12,4},... | collective-permute-start | bytes 3145736 | tf_op jit(solution)/shard_map/ppermute | solution.py:258
  22.3 34.0 %all-to-all-start = ((bf16[64,16,512]{2,1,0:T(8,128)(2,1)}), bf16[64,16,512]{2,1,0:T(8,128)(2,1)S(1)}, u32[]{:S(2)}, u32[]{:S(2)}) async-start(bf16[64,16,512]{2,1,0:T(8,128)(2,1)} %broadcast_in_dim.10), calls=%async_computation | async-start | bytes 2097152 | tf_op jit(solution)/shard_map/all_to_all | solution.py:250
  56.3 1.4 copy-start.1
  56.3 1.1 copy-start.5
  57.7 21.0 %copy-start.3 = (bf16[640,640]{1,0:T(8,128)(2,1)S(1)}, bf16[640,640]{1,0:T(8,128)(2,1)}, u32[]{:S(2)}) copy-start(bf16[640,640]{1,0:T(8,128)(2,1)} %param.30) | copy-start | bytes 2457604
  67.8 48.9 %all-to-all-start.1 = ((bf16[64,16,512]{2,1,0:T(8,128)(2,1)}), bf16[64,16,512]{2,1,0:T(8,128)(2,1)S(1)}, u32[]{:S(2)}, u32[]{:S(2)}) async-start(bf16[64,16,512]{2,1,0:T(8,128)(2,1)} %bitcast.29), calls=%async_computation.1 | async-start | bytes 2097152 | tf_op jit(solution)/shard_map/all_to_all | solution.py:271
  116.7 1.0 copy-start.2
  138.4 10.9 %all-to-all-start.2 = ((f32[8,2,128]{2,1,0:T(2,128)}), f32[8,2,128]{2,1,0:T(2,128)S(1)}, u32[]{:S(2)}, u32[]{:S(2)}) async-start(f32[8,2,128]{2,1,0:T(2,128)} %shard_map.169), calls=%async_computation.2 | async-start | bytes 16384 | tf_op jit(solution)/shard_map/all_to_all | solution.py:275
Sparse Core Ops, SparseCore 0:
  10.3 101.8 all-gather.1

commit v4 on v2

--- a/solution.py
+++ b/solution.py
@@ -24,12 +24,11 @@
     return jnp.dot(a, b, preferred_element_type=F32)
 
 
-def encode_kernel(ids_ref, lens_ref, table_ref, phrase_w_ref, key_w_ref, value_w_ref, k_ref, v_ref):
+def encode_kernel(ids_ref, table_ref, phrase_w_ref, key_w_ref, value_w_ref, k_ref, v_ref):
     rows, tokens = ids_ref.shape
     vocab = table_ref.shape[0]
-    lens = lens_ref[...]
-    slot = lax.broadcasted_iota(jnp.int32, (rows, tokens), 1)
-    ids = jnp.where(slot < lens, ids_ref[...], -1)
+    ids = ids_ref[...]
+    lens = jnp.sum(jnp.where(ids >= 0, 1.0, 0.0), 1, keepdims=True)
     lane = lax.broadcasted_iota(jnp.int32, (rows, 128), 1)
     blocks, units = [], []
     for t in range(tokens):
@@ -46,13 +45,13 @@
                 count += jnp.where(blocks[t] == BF(block), units[t], zero)
             counts.append(count)
         summed += mm(jnp.concatenate(counts, 1), table_ref[pair * 256 : (pair + 1) * 256, :])
-    mean = (summed / lens.astype(F32)).astype(BF)
+    mean = (summed / lens).astype(BF)
     vec = jnp.tanh(mm(mean, phrase_w_ref[...])).astype(BF)
     k_ref[...] = mm(vec, key_w_ref[...]).astype(BF)
     v_ref[...] = mm(vec, value_w_ref[...]).astype(BF)
 
 
-def encode(ids, lens, table, phrase_w, key_w, value_w):
+def encode(ids, table, phrase_w, key_w, value_w):
     phrases, tokens = ids.shape
     vocab, width = table.shape
     tile = 256
@@ -62,7 +61,6 @@
         grid=(phrases // tile,),
         in_specs=[
             pl.BlockSpec((tile, tokens), lambda i: (i, 0)),
-            pl.BlockSpec((tile, 1), lambda i: (i, 0)),
             whole(table),
             whole(phrase_w),
             whole(key_w),
@@ -75,12 +73,13 @@
             bytes_accessed=2 * vocab * width,
             transcendentals=phrases * width,
         ),
-    )(ids, lens.reshape(-1, 1), table, phrase_w, key_w, value_w)
-
-
-def attend_kernel(used, scale, q_ref, k_ref, v_ref, o_ref):
+    )(ids, table, phrase_w, key_w, value_w)
+
+
+def attend_kernel(used, scale, q_ref, k0_ref, v0_ref, k1_ref, v1_ref, o_ref):
     rows, tile = q_ref.shape[0], 256
-    k, v = k_ref[...], v_ref[...]
+    k = jnp.concatenate([k0_ref[...], k1_ref[...]], 0)
+    v = jnp.concatenate([v0_ref[...], v1_ref[...]], 0)
     head = v.shape[1]
     v_ones = jnp.concatenate([v, jnp.ones_like(v)], 1)
     for start in range(0, rows, tile):
@@ -105,26 +104,29 @@
         o_ref[start : start + tile, :] = part.reshape(tile, shape[2]).astype(BF)
 
 
-def attend(asked, keys, values, used):
+def attend(asked, keys, values, other_keys, other_values, used):
     rows, width = asked.shape
     head = width // HEADS
     phrases = keys.shape[0]
+    part = pl.BlockSpec((phrases, head), lambda h: (0, h))
     return pl.pallas_call(
         functools.partial(attend_kernel, used, 1.0 / math.sqrt(head)),
         grid=(HEADS,),
         in_specs=[
             pl.BlockSpec((rows, head), lambda h: (0, h)),
-            pl.BlockSpec((phrases, head), lambda h: (0, h)),
-            pl.BlockSpec((phrases, head), lambda h: (0, h)),
+            part,
+            part,
+            part,
+            part,
         ],
         out_specs=pl.BlockSpec((rows, head), lambda h: (0, h)),
         out_shape=jax.ShapeDtypeStruct((rows, width), BF),
         cost_estimate=pl.CostEstimate(
-            flops=4 * rows * phrases * width,
-            bytes_accessed=4 * rows * width + 4 * phrases * width,
-            transcendentals=rows * phrases * HEADS,
+            flops=8 * rows * phrases * width,
+            bytes_accessed=4 * rows * width + 8 * phrases * width,
+            transcendentals=2 * rows * phrases * HEADS,
         ),
-    )(asked, keys, values)
+    )(asked, keys, values, other_keys, other_values)
 
 
 def join_kernel(used, parts_ref, frames_ref, context_w_ref, joint_w_ref, o_ref):
@@ -252,9 +254,10 @@
     )
 
     swap = [(0, 1), (1, 0)]
-    ids = jnp.concatenate([phrase_ids, lax.ppermute(phrase_ids, "c", swap)], 0)
-    lens = jnp.concatenate([phrase_lens, lax.ppermute(phrase_lens, "c", swap)], 0)
-    keys, values = encode(ids, lens, phrase_table, phrase_w, key_w, value_w)
+    slot = jnp.arange(phrase_ids.shape[1], dtype=jnp.int32)
+    ids = jnp.where(slot[None, :] < phrase_lens[:, None], phrase_ids, -1)
+    keys, values = encode(ids, phrase_table, phrase_w, key_w, value_w)
+    other_keys, other_values = lax.ppermute(keys, "c", swap), lax.ppermute(values, "c", swap)
 
     utts, positions = labels.shape
     frames_dev = used * n_vocab
@@ -270,7 +273,7 @@
     column = vocab_index * cols + jnp.arange(cols, dtype=jnp.int32)
     label_w = mm((own_labels[:, None] == column[None, :]).astype(BF), out_wt).astype(BF)
 
-    parts = attend(asked.reshape(n_peers * PAD, -1), keys, values, used)
+    parts = attend(asked.reshape(n_peers * PAD, -1), keys, values, other_keys, other_values, used)
     parts = lax.all_to_all(parts.reshape(n_peers, PAD, -1), PEERS, 0, 0, tiled=True)
     enc = join(parts, frames_pad, context_w, joint_enc_w, used, n_vocab)
     enc_all = lax.all_to_all(enc, VOCAB, 0, 0, tiled=True)

time: 118 us -> 112 us (0.949)
  waiting for transfers between devices: 24 us -> 30.4 us
  Pallas kernels: 40.2 us -> 34.2 us
  starting transfers between devices: 29.3 us -> 24.7 us
  local copies, waits for them, and re-layouts: 15.5 us -> 13.6 us
    pallas_call x1, Pallas kernels: 15.1 us -> 8.91 us  [encode(): pl.pallas_call(encode_kernel, grid=(phrases // tile,), in_specs=[pl.Block...]
    all_to_all x1, waiting for transfers between devices: 0.01 us -> 4.62 us  [local(): lax.all_to_all(jnp.broadcast_to(queries[None], (n_peers,) + queries.shape...]
    all_to_all x1, starting transfers between devices: 10.4 us -> 6 us  [local(): lax.all_to_all(parts.reshape(n_peers, PAD, -1), PEERS, 0, 0, tiled=True)]
    ppermute x2, waiting for transfers between devices: 0.01 us -> 1.74 us  [the longest x1 1 us: local(): lax.ppermute(keys, 'c', swap)]
    select_n x0 -> x1, other arithmetic: none -> 1.54 us  [local(): ids = jnp.where(slot[None, :] < phrase_lens[:, None], phrase_ids, -1)]
    concatenate x2 -> x0, other arithmetic: 1.41 us -> none  [the longest x1 0.72 us: local(): ids = jnp.concatenate([phrase_ids, lax.ppermute(phrase_ids, 'c', swap)], 0)]
    unnamed x17 -> x24, local copies, waits for them, and re-layouts: 4.94 us -> 5.81 us
  transfers between devices with their start and end apart: 6 -> 6, of which waited for: 3 -> 6; matrix products, arithmetic and copies ran while one was open for 13% -> 12% of each run, Pallas kernels for 13% -> 8%
where the time goes in v4:
time: 112 us; the launch traced here: 111 us
  Pallas kernels  34.2 us (31%)
  waiting for transfers between devices  30.4 us (27%)
  starting transfers between devices  24.7 us (22%)
  local copies, waits for them, and re-layouts  13.6 us (12%)
  other arithmetic  3.69 us (3%)
  matrix products  3.39 us (3%)
    all_to_all x1, waiting for transfers between devices, local(): lax.all_to_all(parts.reshape(n_peers, PAD, -1), PEERS, 0, 0, tiled=True)  13 us
    all_to_all x1, starting transfers between devices, local(): lax.all_to_all(jnp.broadcast_to(queries[None], (n_peers,) + queries.shape...  11.5 us
    pallas_call x1, Pallas kernels, joint(): pl.pallas_call(functools.partial(joint_kernel, used), grid=(n_vocab,), in...  11.2 us
    pallas_call x1, Pallas kernels, attend(): pl.pallas_call(functools.partial(attend_kernel, used, 1.0 / math.sqrt(hea...  9.96 us
    pallas_call x1, Pallas kernels, encode(): pl.pallas_call(encode_kernel, grid=(phrases // tile,), in_specs=[pl.Block...  8.91 us
    all_to_all x1, waiting for transfers between devices, local(): stats = lax.all_to_all(stats, VOCAB, 0, 0, tiled=True)  7.07 us
    all_to_all x1, starting transfers between devices, local(): lax.all_to_all(parts.reshape(n_peers, PAD, -1), PEERS, 0, 0, tiled=True)  6 us
    unnamed x24, local copies, waits for them, and re-layouts  5.81 us
  transfers between devices with their start and end apart: 6, of which 6 were waited for; matrix products, arithmetic and copies ran while one was open for 12% of the time, Pallas kernels for 8%

profile of v4, /device:TPU:0, one launch (start us, length us, event | category | flops | bytes accessed | tf_op | source)
XLA Modules:
  0.0 110.8 jit_solution(14304139557104302049)
XLA Ops:
  0.6 1.2 %copy-done = bf16[1024,512]{1,0:T(8,128)(2,1)S(1)} copy-done((bf16[1024,512]{1,0:T(8,128)(2,1)S(1)}, bf16[1024,512]{1,0:T(8,128)(2,1)}, u32[]{:S(2)}) %copy-start) | copy-done | bytes 1048600
  1.9 1.0 convolution_convert_fusion.2
  2.9 1.1 %broadcast_in_dim.10 = bf16[64,16,512]{2,1,0:T(8,128)(2,1)} broadcast(bf16[16,512]{1,0:T(8,128)(2,1)S(1)} %convolution_convert_fusion.2), dimensions={1,2} | broadcast | bytes 1064960 | tf_op jit(solution)/shard_map/broadcast_in_dim | solution.py:253
  4.0 11.5 %all-to-all-start = ((bf16[64,16,512]{2,1,0:T(8,128)(2,1)}), bf16[64,16,512]{2,1,0:T(8,128)(2,1)S(1)}, u32[]{:S(2)}, u32[]{:S(2)}) async-start(bf16[64,16,512]{2,1,0:T(8,128)(2,1)} %broadcast_in_dim.10), calls=%async_computation | async-start | bytes 2097152 | tf_op jit(solution)/shard_map/all_to_all | solution.py:252
  15.5 0.8 copy.20
  16.3 1.5 %fusion.2.ids_ref = s32[512,8]{1,0:T(8,128)} fusion(s32[512,8]{1,0:T(8,128)S(1)} %copy.20, s32[512]{0:T(512)} %param.21), kind=kLoop, calls=%fused_computation.7 | loop fusion | flops 8192 | bytes 34816 | tf_op jit(solution)/shard_map/jit(_where)/select_n | solution.py:258
  17.9 8.9 %shard_map.167 = (bf16[512,512]{1,0:T(8,128)(2,1)}, bf16[512,512]{1,0:T(8,128)(2,1)}) custom-call(s32[512,8]{1,0:T(8,128)} %fusion.2.ids_ref, bf16[4096,512]{1,0:T(8,128)(2,1)} %table_ref.1, bf16[512,512]{1,0:T(8,128)(2,1)} %phrase_w_ref.1, bf16[512,512]{1,0:T(8,128)(2,1)} %key_w_ref.1, bf16[512,512]{1,0:T(8,128)(2,1)} %value_w_ref.1), custom_call_target="tpu_custom_call" | custom-call | flops 42949672960 | bytes 4194304 | tf_op jit(solution)/shard_map/pallas_call | solution.py:59
  27.3 0.6 pad.8.frames_ref
  27.9 1.0 collective-permute-done.k1_ref
  28.9 0.7 collective-permute-done.1.v1_ref
  29.7 4.6 %all-to-all-done = bf16[64,16,512]{2,1,0:T(8,128)(2,1)S(1)} async-done(((bf16[64,16,512]{2,1,0:T(8,128)(2,1)}), bf16[64,16,512]{2,1,0:T(8,128)(2,1)S(1)}, u32[]{:S(2)}, u32[]{:S(2)}) %all-to-all-start) | async-done | bytes 1048608 | tf_op jit(solution)/shard_map/all_to_all | solution.py:252
  34.3 1.0 copy-done.3
  35.3 10.0 %shard_map.168 = bf16[1024,512]{1,0:T(8,128)(2,1)} custom-call(bf16[1024,512]{1,0:T(8,128)(2,1)} %bitcast.27, bf16[512,512]{1,0:T(8,128)(2,1)} %get-tuple-element.4.k0_ref, bf16[512,512]{1,0:T(8,128)(2,1)} %get-tuple-element.5.v0_ref, bf16[512,512]{1,0:T(8,128)(2,1)} %copy-done.6, bf16[512,512]{1,0:T(8,128)(2,1)} %copy-done.7), custom_call_target="tpu_custom_call" | custom-call | flops 2147483648 | bytes 4194304 | tf_op jit(solution)/shard_map/pallas_call | solution.py:112
  45.3 6.0 %all-to-all-start.1 = ((bf16[64,16,512]{2,1,0:T(8,128)(2,1)}), bf16[64,16,512]{2,1,0:T(8,128)(2,1)S(1)}, u32[]{:S(2)}, u32[]{:S(2)}) async-start(bf16[64,16,512]{2,1,0:T(8,128)(2,1)} %bitcast.28), calls=%async_computation.1 | async-start | bytes 2097152 | tf_op jit(solution)/shard_map/all_to_all | solution.py:277
  51.4 3.9 %gather_fusion = bf16[64,640]{1,0:T(8,128)(2,1)S(1)} fusion(bf16[4096,640]{1,0:T(8,128)(2,1)} %param.29, s32[1024]{0:T(1024)S(1)} %pad_clamp_fusion), kind=kCustom, calls=%fused_computation | custom fusion | bytes 164096 | tf_op jit(solution)/shard_map/gather | solution.py:269
  55.3 2.1 %fusion.pred_ref = f32[64,640]{1,0:T(8,128)} fusion(bf16[64,640]{1,0:T(8,128)(2,1)S(1)} %gather_fusion, bf16[640,640]{1,0:T(8,128)(2,1)} %param.30), kind=kOutput, calls=%fused_computation.3 | convolution fusion | flops 52510720 | bytes 1064960 | tf_op jit(solution)/shard_map/dot_general | solution.py:24
  57.4 13.0 %all-to-all-done.1.parts_ref = bf16[64,16,512]{2,1,0:T(8,128)(2,1)S(1)} async-done(((bf16[64,16,512]{2,1,0:T(8,128)(2,1)}), bf16[64,16,512]{2,1,0:T(8,128)(2,1)S(1)}, u32[]{:S(2)}, u32[]{:S(2)}) %all-to-all-start.1) | async-done | bytes 1048608 | tf_op jit(solution)/shard_map/all_to_all | solution.py:277
  70.4 1.0 copy-done.1
  71.3 4.1 %shard_map.169 = bf16[8,16,640]{2,1,0:T(8,128)(2,1)} custom-call(bf16[64,16,512]{2,1,0:T(8,128)(2,1)} %copy-done.1, bf16[16,1024]{1,0:T(8,128)(2,1)} %pad.8.frames_ref, bf16[512,1024]{1,0:T(8,128)(2,1)} %context_w_ref.1, bf16[1024,640]{1,0:T(8,128)(2,1)} %joint_w_ref.1), custom_call_target="tpu_custom_call" | custom-call | tf_op jit(solution)/shard_map/pallas_call | solution.py:153
  75.4 3.4 %all-to-all-start.2 = ((bf16[8,16,640]{2,1,0:T(8,128)(2,1)}), bf16[8,16,640]{2,1,0:T(8,128)(2,1)S(1)}, u32[]{:S(2)}, u32[]{:S(2)}) async-start(bf16[8,16,640]{2,1,0:T(8,128)(2,1)} %shard_map.169), calls=%async_computation.2 | async-start | bytes 327680 | tf_op jit(solution)/shard_map/all_to_all | solution.py:279
  79.1 1.1 copy.21
  80.2 0.7 pad.9.label_w_ref
  80.9 0.6 dynamic_slice.9
  81.5 0.6 dynamic_slice.10
  82.1 0.7 fusion.9
  82.7 4.0 %all-to-all-done.2.enc_ref = bf16[8,16,640]{2,1,0:T(8,128)(2,1)S(1)} async-done(((bf16[8,16,640]{2,1,0:T(8,128)(2,1)}), bf16[8,16,640]{2,1,0:T(8,128)(2,1)S(1)}, u32[]{:S(2)}, u32[]{:S(2)}) %all-to-all-start.2) | async-done | bytes 163872 | tf_op jit(solution)/shard_map/all_to_all | solution.py:279
  86.8 0.7 copy-done.4
  87.4 11.2 %shard_map.170 = f32[8,24,128]{2,1,0:T(8,128)} custom-call(bf16[8,16,640]{2,1,0:T(8,128)(2,1)} %copy-done.4, f32[64,640]{1,0:T(8,128)} %fusion.pred_ref, bf16[512,640]{1,0:T(8,128)(2,1)} %bitcast.29, bf16[8,16,640]{2,1,0:T(8,128)(2,1)} %pad.9.label_w_ref), custom_call_target="tpu_custom_call" | custom-call | flops 4026531840 | bytes 655360 | tf_op jit(solution)/shard_map/pallas_call | solution.py:208
  98.7 3.4 %all-to-all-start.3 = ((f32[8,24,128]{2,1,0:T(8,128)}), f32[8,24,128]{2,1,0:T(8,128)S(1)}, u32[]{:S(2)}, u32[]{:S(2)}) async-start(f32[8,24,128]{2,1,0:T(8,128)} %shard_map.170), calls=%async_computation.3 | async-start | bytes 196608 | tf_op jit(solution)/shard_map/all_to_all | solution.py:281
  102.0 0.7 add_compare_fusion
  102.7 7.1 %all-to-all-done.3 = f32[8,24,128]{2,1,0:T(8,128)S(1)} async-done(((f32[8,24,128]{2,1,0:T(8,128)}), f32[8,24,128]{2,1,0:T(8,128)S(1)}, u32[]{:S(2)}, u32[]{:S(2)}) %all-to-all-start.3) | async-done | bytes 98336 | tf_op jit(solution)/shard_map/all_to_all | solution.py:281
  110.1 0.7 select_bitcast_fusion
  (35 shorter events, 1.3 us)
Async XLA Ops:
  0.6 1.2 %copy-start = (bf16[1024,512]{1,0:T(8,128)(2,1)S(1)}, bf16[1024,512]{1,0:T(8,128)(2,1)}, u32[]{:S(2)}) copy-start(bf16[1024,512]{1,0:T(8,128)(2,1)} %param.26) | copy-start | bytes 3145732
  4.0 30.3 %all-to-all-start = ((bf16[64,16,512]{2,1,0:T(8,128)(2,1)}), bf16[64,16,512]{2,1,0:T(8,128)(2,1)S(1)}, u32[]{:S(2)}, u32[]{:S(2)}) async-start(bf16[64,16,512]{2,1,0:T(8,128)(2,1)} %broadcast_in_dim.10), calls=%async_computation | async-start | bytes 2097152 | tf_op jit(solution)/shard_map/all_to_all | solution.py:252
  17.9 9.4 %copy-start.5 = (bf16[12,1024]{1,0:T(8,128)(2,1)S(1)}, bf16[12,1024]{1,0:T(8,128)(2,1)}, u32[]{:S(2)}) copy-start(bf16[12,1024]{1,0:T(8,128)(2,1)} %param.16) | copy-start | bytes 73732
  26.8 24.5 %copy-start.8 = (s32[4,64]{1,0:T(4,128)S(1)}, s32[4,64]{1,0:T(4,128)}, u32[]{:S(2)}) copy-start(s32[4,64]{1,0:T(4,128)} %param.18) | copy-start | bytes 3076
  26.8 2.1 %collective-permute-start = (bf16[512,512]{1,0:T(8,128)(2,1)}, bf16[512,512]{1,0:T(8,128)(2,1)S(1)}, u32[]{:S(2)}, u32[]{:S(2)}) collective-permute-start(bf16[512,512]{1,0:T(8,128)(2,1)} %get-tuple-element.4.k0_ref), channel_id=1, source_target_pairs={{0,8},{8,0},{1,9},{9,1},{2,10},{10,2},{3,11},{11,3},{4,12},{12,4},... | collective-permute-start | bytes 1572872 | tf_op jit(solution)/shard_map/ppermute | solution.py:260
  26.8 2.9 %collective-permute-start.1 = (bf16[512,512]{1,0:T(8,128)(2,1)}, bf16[512,512]{1,0:T(8,128)(2,1)S(1)}, u32[]{:S(2)}, u32[]{:S(2)}) collective-permute-start(bf16[512,512]{1,0:T(8,128)(2,1)} %get-tuple-element.5.v0_ref), channel_id=1, source_target_pairs={{0,8},{8,0},{1,9},{9,1},{2,10},{10,2},{3,11},{11,3},{4,12},{12,4},... | collective-permute-start | bytes 1572872 | tf_op jit(solution)/shard_map/ppermute | solution.py:260
  28.9 5.4 %copy-start.6 = (bf16[512,512]{1,0:T(8,128)(2,1)}, bf16[512,512]{1,0:T(8,128)(2,1)S(1)}, u32[]{:S(2)}) copy-start(bf16[512,512]{1,0:T(8,128)(2,1)S(1)} %collective-permute-done.k1_ref) | copy-start | bytes 1572868
  29.7 4.6 %copy-start.7 = (bf16[512,512]{1,0:T(8,128)(2,1)}, bf16[512,512]{1,0:T(8,128)(2,1)S(1)}, u32[]{:S(2)}) copy-start(bf16[512,512]{1,0:T(8,128)(2,1)S(1)} %collective-permute-done.1.v1_ref) | copy-start | bytes 1572868
  34.3 1.0 copy-start.3
  45.2 33.6 %copy-start.2 = (bf16[640,512]{1,0:T(8,128)(2,1)S(1)}, bf16[640,512]{1,0:T(8,128)(2,1)}, u32[]{:S(2)}) copy-start(bf16[640,512]{1,0:T(8,128)(2,1)} %param.31) | copy-start | bytes 1966084
  45.2 35.7 %copy-start.9 = (s32[4]{0:T(128)S(1)}, s32[4]{0:T(128)}, u32[]{:S(2)}) copy-start(s32[4]{0:T(128)} %param.17) | copy-start | bytes 52
  45.2 36.2 %copy-start.10 = (s32[4]{0:T(128)S(1)}, s32[4]{0:T(128)}, u32[]{:S(2)}) copy-start(s32[4]{0:T(128)} %param.19) | copy-start | bytes 52
  45.3 25.1 %all-to-all-start.1 = ((bf16[64,16,512]{2,1,0:T(8,128)(2,1)}), bf16[64,16,512]{2,1,0:T(8,128)(2,1)S(1)}, u32[]{:S(2)}, u32[]{:S(2)}) async-start(bf16[64,16,512]{2,1,0:T(8,128)(2,1)} %bitcast.28), calls=%async_computation.1 | async-start | bytes 2097152 | tf_op jit(solution)/shard_map/all_to_all | solution.py:277
  70.4 1.0 copy-start.1
  75.4 11.4 %all-to-all-start.2 = ((bf16[8,16,640]{2,1,0:T(8,128)(2,1)}), bf16[8,16,640]{2,1,0:T(8,128)(2,1)S(1)}, u32[]{:S(2)}, u32[]{:S(2)}) async-start(bf16[8,16,640]{2,1,0:T(8,128)(2,1)} %shard_map.169), calls=%async_computation.2 | async-start | bytes 327680 | tf_op jit(solution)/shard_map/all_to_all | solution.py:279
  86.8 0.7 copy-start.4
  98.7 11.1 %all-to-all-start.3 = ((f32[8,24,128]{2,1,0:T(8,128)}), f32[8,24,128]{2,1,0:T(8,128)S(1)}, u32[]{:S(2)}, u32[]{:S(2)}) async-start(f32[8,24,128]{2,1,0:T(8,128)} %shard_map.170), calls=%async_computation.3 | async-start | bytes 196608 | tf_op jit(solution)/shard_map/all_to_all | solution.py:281

commit v5 on v4

--- a/solution.py
+++ b/solution.py
@@ -150,8 +150,12 @@
 
 
 def join(parts, frames, context_w, joint_w, used, copies):
+    parts = pltpu.with_memory_space_constraint(parts, pltpu.VMEM)
+    vmem = pl.BlockSpec(memory_space=pltpu.VMEM)
     return pl.pallas_call(
         functools.partial(join_kernel, used),
+        in_specs=[vmem] * 4,
+        out_specs=vmem,
         out_shape=jax.ShapeDtypeStruct((copies, frames.shape[0], joint_w.shape[1]), BF),
     )(parts, frames, context_w, joint_w)
 
@@ -204,12 +208,13 @@
     cols = out_wt.shape[0]
     pairs = own * frames
     stat = 8
+    enc_all = pltpu.with_memory_space_constraint(enc_all, pltpu.VMEM)
     label_w = jnp.pad(label_w.reshape(n_vocab, own, width), ((0, 0), (0, 16 - own), (0, 0)))
     return pl.pallas_call(
         functools.partial(joint_kernel, used),
         grid=(n_vocab,),
         in_specs=[
-            pl.BlockSpec((groups, pad, width), lambda i: (0, 0, 0)),
+            pl.BlockSpec(memory_space=pltpu.VMEM),
             pl.BlockSpec((own, width), lambda i: (i, 0)),
             pl.BlockSpec((cols, width), lambda i: (0, 0)),
             pl.BlockSpec((1, 16, width), lambda i: (i, 0, 0)),

time: 112 us -> 110 us (0.982)
  local copies, waits for them, and re-layouts: 13.6 us -> 11.9 us
    unnamed x24 -> x20, local copies, waits for them, and re-layouts: 5.81 us -> 4.17 us
  transfers between devices with their start and end apart: 6 -> 6, of which waited for: 6 -> 6; matrix products, arithmetic and copies ran while one was open for 12% -> 13% of each run, Pallas kernels for 8% -> 8%
where the time goes in v5:
time: 110 us; the launch traced here: 109 us
  Pallas kernels  33.7 us (31%)
  waiting for transfers between devices  30.5 us (28%)
  starting transfers between devices  24.7 us (22%)
  local copies, waits for them, and re-layouts  11.9 us (11%)
  other arithmetic  3.68 us (3%)
  matrix products  3.38 us (3%)
    all_to_all x1, waiting for transfers between devices, local(): lax.all_to_all(parts.reshape(n_peers, PAD, -1), PEERS, 0, 0, tiled=True)  13 us
    all_to_all x1, starting transfers between devices, local(): lax.all_to_all(jnp.broadcast_to(queries[None], (n_peers,) + queries.shape...  11.5 us
    pallas_call x1, Pallas kernels, joint(): pl.pallas_call(functools.partial(joint_kernel, used), grid=(n_vocab,), in...  11.1 us
    pallas_call x1, Pallas kernels, attend(): pl.pallas_call(functools.partial(attend_kernel, used, 1.0 / math.sqrt(hea...  9.94 us
    pallas_call x1, Pallas kernels, encode(): pl.pallas_call(encode_kernel, grid=(phrases // tile,), in_specs=[pl.Block...  8.91 us
    all_to_all x1, waiting for transfers between devices, local(): stats = lax.all_to_all(stats, VOCAB, 0, 0, tiled=True)  7.07 us
    all_to_all x1, starting transfers between devices, local(): lax.all_to_all(parts.reshape(n_peers, PAD, -1), PEERS, 0, 0, tiled=True)  5.96 us
    all_to_all x1, waiting for transfers between devices, local(): lax.all_to_all(jnp.broadcast_to(queries[None], (n_peers,) + queries.shape...  4.64 us
  transfers between devices with their start and end apart: 6, of which 6 were waited for; matrix products, arithmetic and copies ran while one was open for 13% of the time, Pallas kernels for 8%

profile of v5, /device:TPU:0, one launch (start us, length us, event | category | flops | bytes accessed | tf_op | source)
XLA Modules:
  0.0 108.7 jit_solution(7999153076565962307)
XLA Ops:
  0.6 1.2 %copy-done = bf16[1024,512]{1,0:T(8,128)(2,1)S(1)} copy-done((bf16[1024,512]{1,0:T(8,128)(2,1)S(1)}, bf16[1024,512]{1,0:T(8,128)(2,1)}, u32[]{:S(2)}) %copy-start) | copy-done | bytes 1048600
  1.9 1.0 convolution_convert_fusion.2
  2.9 1.1 %broadcast_in_dim.10 = bf16[64,16,512]{2,1,0:T(8,128)(2,1)} broadcast(bf16[16,512]{1,0:T(8,128)(2,1)S(1)} %convolution_convert_fusion.2), dimensions={1,2} | broadcast | bytes 1064960 | tf_op jit(solution)/shard_map/broadcast_in_dim | solution.py:258
  4.0 11.5 %all-to-all-start = ((bf16[64,16,512]{2,1,0:T(8,128)(2,1)}), bf16[64,16,512]{2,1,0:T(8,128)(2,1)S(1)}, u32[]{:S(2)}, u32[]{:S(2)}) async-start(bf16[64,16,512]{2,1,0:T(8,128)(2,1)} %broadcast_in_dim.10), calls=%async_computation | async-start | bytes 2097152 | tf_op jit(solution)/shard_map/all_to_all | solution.py:257
  15.5 0.8 copy.20
  16.3 1.5 %fusion.2.ids_ref = s32[512,8]{1,0:T(8,128)} fusion(s32[512,8]{1,0:T(8,128)S(1)} %copy.20, s32[512]{0:T(512)} %param.21), kind=kLoop, calls=%fused_computation.7 | loop fusion | flops 8192 | bytes 34816 | tf_op jit(solution)/shard_map/jit(_where)/select_n | solution.py:263
  17.9 8.9 %shard_map.167 = (bf16[512,512]{1,0:T(8,128)(2,1)}, bf16[512,512]{1,0:T(8,128)(2,1)}) custom-call(s32[512,8]{1,0:T(8,128)} %fusion.2.ids_ref, bf16[4096,512]{1,0:T(8,128)(2,1)} %table_ref.1, bf16[512,512]{1,0:T(8,128)(2,1)} %phrase_w_ref.1, bf16[512,512]{1,0:T(8,128)(2,1)} %key_w_ref.1, bf16[512,512]{1,0:T(8,128)(2,1)} %value_w_ref.1), custom_call_target="tpu_custom_call" | custom-call | flops 42949672960 | bytes 4194304 | tf_op jit(solution)/shard_map/pallas_call | solution.py:59
  26.8 0.5 collective-permute-start.1
  27.3 0.6 pad.8.frames_ref
  27.9 1.0 collective-permute-done.k1_ref
  28.9 0.7 collective-permute-done.1.v1_ref
  29.6 4.6 %all-to-all-done = bf16[64,16,512]{2,1,0:T(8,128)(2,1)S(1)} async-done(((bf16[64,16,512]{2,1,0:T(8,128)(2,1)}), bf16[64,16,512]{2,1,0:T(8,128)(2,1)S(1)}, u32[]{:S(2)}, u32[]{:S(2)}) %all-to-all-start) | async-done | bytes 1048608 | tf_op jit(solution)/shard_map/all_to_all | solution.py:257
  34.3 1.0 copy-done.2
  35.3 9.9 %shard_map.168 = bf16[1024,512]{1,0:T(8,128)(2,1)} custom-call(bf16[1024,512]{1,0:T(8,128)(2,1)} %bitcast.27, bf16[512,512]{1,0:T(8,128)(2,1)} %get-tuple-element.4.k0_ref, bf16[512,512]{1,0:T(8,128)(2,1)} %get-tuple-element.5.v0_ref, bf16[512,512]{1,0:T(8,128)(2,1)} %copy-done.4, bf16[512,512]{1,0:T(8,128)(2,1)} %copy-done.5), custom_call_target="tpu_custom_call" | custom-call | flops 2147483648 | bytes 4194304 | tf_op jit(solution)/shard_map/pallas_call | solution.py:112
  45.2 6.0 %all-to-all-start.1 = ((bf16[64,16,512]{2,1,0:T(8,128)(2,1)}), bf16[64,16,512]{2,1,0:T(8,128)(2,1)S(1)}, u32[]{:S(2)}, u32[]{:S(2)}) async-start(bf16[64,16,512]{2,1,0:T(8,128)(2,1)} %bitcast.28), calls=%async_computation.1 | async-start | bytes 2097152 | tf_op jit(solution)/shard_map/all_to_all | solution.py:282
  51.3 3.9 %gather_fusion = bf16[64,640]{1,0:T(8,128)(2,1)S(1)} fusion(bf16[4096,640]{1,0:T(8,128)(2,1)} %param.29, s32[1024]{0:T(1024)S(1)} %pad_clamp_fusion), kind=kCustom, calls=%fused_computation | custom fusion | bytes 164096 | tf_op jit(solution)/shard_map/gather | solution.py:274
  55.3 2.1 %fusion.pred_ref = f32[64,640]{1,0:T(8,128)} fusion(bf16[64,640]{1,0:T(8,128)(2,1)S(1)} %gather_fusion, bf16[640,640]{1,0:T(8,128)(2,1)} %param.30), kind=kOutput, calls=%fused_computation.3 | convolution fusion | flops 52510720 | bytes 1064960 | tf_op jit(solution)/shard_map/dot_general | solution.py:24
  57.3 13.0 %all-to-all-done.1.parts_ref = bf16[64,16,512]{2,1,0:T(8,128)(2,1)S(1)} async-done(((bf16[64,16,512]{2,1,0:T(8,128)(2,1)}), bf16[64,16,512]{2,1,0:T(8,128)(2,1)S(1)}, u32[]{:S(2)}, u32[]{:S(2)}) %all-to-all-start.1) | async-done | bytes 1048608 | tf_op jit(solution)/shard_map/all_to_all | solution.py:282
  70.3 3.7 %shard_map.169 = bf16[8,16,640]{2,1,0:T(8,128)(2,1)} custom-call(bf16[64,16,512]{2,1,0:T(8,128)(2,1)S(1)} %all-to-all-done.1.parts_ref, bf16[16,1024]{1,0:T(8,128)(2,1)} %pad.8.frames_ref, bf16[512,1024]{1,0:T(8,128)(2,1)} %context_w_ref.1, bf16[1024,640]{1,0:T(8,128)(2,1)} %joint_w_ref.1), custom_call_target="tpu_custom_call" | custom-call | tf_op jit(solution)/shard_map/pallas_call | solution.py:155
  74.1 3.4 %all-to-all-start.2 = ((bf16[8,16,640]{2,1,0:T(8,128)(2,1)}), bf16[8,16,640]{2,1,0:T(8,128)(2,1)S(1)}, u32[]{:S(2)}, u32[]{:S(2)}) async-start(bf16[8,16,640]{2,1,0:T(8,128)(2,1)} %shard_map.169), calls=%async_computation.2 | async-start | bytes 327680 | tf_op jit(solution)/shard_map/all_to_all | solution.py:284
  77.5 0.3 fusion.1
  77.8 1.1 copy.21
  78.9 0.7 pad.9.label_w_ref
  79.5 0.6 dynamic_slice.9
  80.1 0.6 dynamic_slice.10
  80.7 0.7 fusion.9
  81.4 4.1 %all-to-all-done.2.enc_ref = bf16[8,16,640]{2,1,0:T(8,128)(2,1)S(1)} async-done(((bf16[8,16,640]{2,1,0:T(8,128)(2,1)}), bf16[8,16,640]{2,1,0:T(8,128)(2,1)S(1)}, u32[]{:S(2)}, u32[]{:S(2)}) %all-to-all-start.2) | async-done | bytes 163872 | tf_op jit(solution)/shard_map/all_to_all | solution.py:284
  85.4 11.1 %shard_map.170 = f32[8,24,128]{2,1,0:T(8,128)} custom-call(bf16[8,16,640]{2,1,0:T(8,128)(2,1)S(1)} %all-to-all-done.2.enc_ref, f32[64,640]{1,0:T(8,128)} %fusion.pred_ref, bf16[512,640]{1,0:T(8,128)(2,1)} %bitcast.29, bf16[8,16,640]{2,1,0:T(8,128)(2,1)} %pad.9.label_w_ref), custom_call_target="tpu_custom_call" | custom-call | flops 4026531840 | bytes 655360 | tf_op jit(solution)/shard_map/pallas_call | solution.py:213
  96.6 3.4 %all-to-all-start.3 = ((f32[8,24,128]{2,1,0:T(8,128)}), f32[8,24,128]{2,1,0:T(8,128)S(1)}, u32[]{:S(2)}, u32[]{:S(2)}) async-start(f32[8,24,128]{2,1,0:T(8,128)} %shard_map.170), calls=%async_computation.3 | async-start | bytes 196608 | tf_op jit(solution)/shard_map/all_to_all | solution.py:286
  99.9 0.7 add_compare_fusion
  100.6 7.1 %all-to-all-done.3 = f32[8,24,128]{2,1,0:T(8,128)S(1)} async-done(((f32[8,24,128]{2,1,0:T(8,128)}), f32[8,24,128]{2,1,0:T(8,128)S(1)}, u32[]{:S(2)}, u32[]{:S(2)}) %all-to-all-start.3) | async-done | bytes 98336 | tf_op jit(solution)/shard_map/all_to_all | solution.py:286
  108.1 0.7 select_bitcast_fusion
  (31 shorter events, 0.5 us)
Async XLA Ops:
  0.6 1.2 %copy-start = (bf16[1024,512]{1,0:T(8,128)(2,1)S(1)}, bf16[1024,512]{1,0:T(8,128)(2,1)}, u32[]{:S(2)}) copy-start(bf16[1024,512]{1,0:T(8,128)(2,1)} %param.26) | copy-start | bytes 3145732
  4.0 30.3 %all-to-all-start = ((bf16[64,16,512]{2,1,0:T(8,128)(2,1)}), bf16[64,16,512]{2,1,0:T(8,128)(2,1)S(1)}, u32[]{:S(2)}, u32[]{:S(2)}) async-start(bf16[64,16,512]{2,1,0:T(8,128)(2,1)} %broadcast_in_dim.10), calls=%async_computation | async-start | bytes 2097152 | tf_op jit(solution)/shard_map/all_to_all | solution.py:257
  17.9 9.4 %copy-start.3 = (bf16[12,1024]{1,0:T(8,128)(2,1)S(1)}, bf16[12,1024]{1,0:T(8,128)(2,1)}, u32[]{:S(2)}) copy-start(bf16[12,1024]{1,0:T(8,128)(2,1)} %param.16) | copy-start | bytes 73732
  26.8 24.4 %copy-start.6 = (s32[4,64]{1,0:T(4,128)S(1)}, s32[4,64]{1,0:T(4,128)}, u32[]{:S(2)}) copy-start(s32[4,64]{1,0:T(4,128)} %param.18) | copy-start | bytes 3076
  26.8 2.1 %collective-permute-start = (bf16[512,512]{1,0:T(8,128)(2,1)}, bf16[512,512]{1,0:T(8,128)(2,1)S(1)}, u32[]{:S(2)}, u32[]{:S(2)}) collective-permute-start(bf16[512,512]{1,0:T(8,128)(2,1)} %get-tuple-element.4.k0_ref), channel_id=1, source_target_pairs={{0,8},{8,0},{1,9},{9,1},{2,10},{10,2},{3,11},{11,3},{4,12},{12,4},... | collective-permute-start | bytes 1572872 | tf_op jit(solution)/shard_map/ppermute | solution.py:265
  26.8 2.9 %collective-permute-start.1 = (bf16[512,512]{1,0:T(8,128)(2,1)}, bf16[512,512]{1,0:T(8,128)(2,1)S(1)}, u32[]{:S(2)}, u32[]{:S(2)}) collective-permute-start(bf16[512,512]{1,0:T(8,128)(2,1)} %get-tuple-element.5.v0_ref), channel_id=1, source_target_pairs={{0,8},{8,0},{1,9},{9,1},{2,10},{10,2},{3,11},{11,3},{4,12},{12,4},... | collective-permute-start | bytes 1572872 | tf_op jit(solution)/shard_map/ppermute | solution.py:265
  28.9 5.4 %copy-start.4 = (bf16[512,512]{1,0:T(8,128)(2,1)}, bf16[512,512]{1,0:T(8,128)(2,1)S(1)}, u32[]{:S(2)}) copy-start(bf16[512,512]{1,0:T(8,128)(2,1)S(1)} %collective-permute-done.k1_ref) | copy-start | bytes 1572868
  29.6 4.6 %copy-start.5 = (bf16[512,512]{1,0:T(8,128)(2,1)}, bf16[512,512]{1,0:T(8,128)(2,1)S(1)}, u32[]{:S(2)}) copy-start(bf16[512,512]{1,0:T(8,128)(2,1)S(1)} %collective-permute-done.1.v1_ref) | copy-start | bytes 1572868
  34.3 1.0 copy-start.2
  45.2 32.2 %copy-start.1 = (bf16[640,512]{1,0:T(8,128)(2,1)S(1)}, bf16[640,512]{1,0:T(8,128)(2,1)}, u32[]{:S(2)}) copy-start(bf16[640,512]{1,0:T(8,128)(2,1)} %param.31) | copy-start | bytes 1966084
  45.2 34.3 %copy-start.7 = (s32[4]{0:T(128)S(1)}, s32[4]{0:T(128)}, u32[]{:S(2)}) copy-start(s32[4]{0:T(128)} %param.17) | copy-start | bytes 52
  45.2 34.9 %copy-start.8 = (s32[4]{0:T(128)S(1)}, s32[4]{0:T(128)}, u32[]{:S(2)}) copy-start(s32[4]{0:T(128)} %param.19) | copy-start | bytes 52
  45.2 25.1 %all-to-all-start.1 = ((bf16[64,16,512]{2,1,0:T(8,128)(2,1)}), bf16[64,16,512]{2,1,0:T(8,128)(2,1)S(1)}, u32[]{:S(2)}, u32[]{:S(2)}) async-start(bf16[64,16,512]{2,1,0:T(8,128)(2,1)} %bitcast.28), calls=%async_computation.1 | async-start | bytes 2097152 | tf_op jit(solution)/shard_map/all_to_all | solution.py:282
  74.1 11.4 %all-to-all-start.2 = ((bf16[8,16,640]{2,1,0:T(8,128)(2,1)}), bf16[8,16,640]{2,1,0:T(8,128)(2,1)S(1)}, u32[]{:S(2)}, u32[]{:S(2)}) async-start(bf16[8,16,640]{2,1,0:T(8,128)(2,1)} %shard_map.169), calls=%async_computation.2 | async-start | bytes 327680 | tf_op jit(solution)/shard_map/all_to_all | solution.py:284
  96.6 11.1 %all-to-all-start.3 = ((f32[8,24,128]{2,1,0:T(8,128)}), f32[8,24,128]{2,1,0:T(8,128)S(1)}, u32[]{:S(2)}, u32[]{:S(2)}) async-start(f32[8,24,128]{2,1,0:T(8,128)} %shard_map.170), calls=%async_computation.3 | async-start | bytes 196608 | tf_op jit(solution)/shard_map/all_to_all | solution.py:286
